TPU v7x, 32 devices: a whole 2x2x4 slice. The times are simulated.
32 devices in a mesh: dp: 4 (over z), seq: 8 (over y, x, core).
Axes of the slice: x: 2, y: 2, z: 4, core: 2. Of those that a mesh axis runs over, the one named last changes fastest.
Arguments:
- hidden_in: bfloat16 [4, 2048, 1024], P('dp', 'seq'), may hold values from -6 to 6
- out_cotangent: bfloat16 [4, 2048, 1024], P('dp', 'seq'), may hold values from -6 to 6
- norm_gain: float32 [1024], P(('dp', 'seq')), may hold values from 0.5 to 1.5
- norm_shift: float32 [1024], P(('dp', 'seq')), may hold values from -1.75 to 1.75
- attend_in: float32 [1024, 3072], P(('dp', 'seq')), may hold values from -0.1875 to 0.1875
- attend_out: float32 [1024, 1024], P(('dp', 'seq')), may hold values from -0.75 to 0.75
- expand_weight: float32 [1024, 4096], P(('dp', 'seq')), may hold values from -0.1875 to 0.1875
- expand_bias: float32 [4096], P(('dp', 'seq')), may hold values from -1.75 to 1.75
- reduce_weight: float32 [4096, 1024], P(('dp', 'seq')), may hold values from -0.09375 to 0.09375
- reduce_bias: float32 [1024], P(('dp', 'seq')), may hold values from -1.75 to 1.75
- gain_moment: float32 [1024], P(('dp', 'seq')), may hold values from -24 to 24
- shift_moment: float32 [1024], P(('dp', 'seq')), may hold values from -24 to 24
- inward_moment: float32 [1024, 3072], P(('dp', 'seq')), may hold values from -24 to 24
- outward_moment: float32 [1024, 1024], P(('dp', 'seq')), may hold values from -24 to 24
- expand_moment: float32 [1024, 4096], P(('dp', 'seq')), may hold values from -24 to 24
- expbias_moment: float32 [4096], P(('dp', 'seq')), may hold values from -24 to 24
- reduce_moment: float32 [4096, 1024], P(('dp', 'seq')), may hold values from -24 to 24
- redbias_moment: float32 [1024], P(('dp', 'seq')), may hold values from -24 to 24
- learn_rate: float32 [1], replicated, may hold values from 0.01 to 0.04
- decay_rate: float32 [1], replicated, may hold values from 0.05 to 0.2
Outputs:
- hidden_out: bfloat16 [4, 2048, 1024], P('dp', 'seq')
- hidden_grad: bfloat16 [4, 2048, 1024], P('dp', 'seq')
- gain_momentum: float32 [1024], P(('dp', 'seq'))
- shift_momentum: float32 [1024], P(('dp', 'seq'))
- inward_momentum: float32 [1024, 3072], P(('dp', 'seq'))
- outward_momentum: float32 [1024, 1024], P(('dp', 'seq'))
- expand_momentum: float32 [1024, 4096], P(('dp', 'seq'))
- expbias_momentum: float32 [4096], P(('dp', 'seq'))
- reduce_momentum: float32 [4096, 1024], P(('dp', 'seq'))
- redbias_momentum: float32 [1024], P(('dp', 'seq'))
- updated_gain: float32 [1024], P(('dp', 'seq'))
- updated_shift: float32 [1024], P(('dp', 'seq'))
- updated_in: float32 [1024, 3072], P(('dp', 'seq'))
- updated_out: float32 [1024, 1024], P(('dp', 'seq'))
- updated_expand: float32 [1024, 4096], P(('dp', 'seq'))
- updated_expbias: float32 [4096], P(('dp', 'seq'))
- updated_reduce: float32 [4096, 1024], P(('dp', 'seq'))
- updated_redbias: float32 [1024], P(('dp', 'seq'))
All inputs are finite; a program needn't handle non-finite values.
Results may differ from a plain program's by a relative error of at most 0.011.
Values may be sent and summed in bfloat16 or wider, within the bound.
A program may use at most 320 MiB of HBM per device.

v0:
```python
import jax
import jax.numpy as jnp
from jax import lax
from jax.sharding import PartitionSpec as P

D = 1024
H = 16
HD = 64
ROT = 32


epsilon = 1e-05
masked_score = -1e30


def rotary(block, positions, direction):
    half_rot = ROT // 2
    frequency = 10000.0 ** (-2.0 * jnp.arange(half_rot, dtype=jnp.float32) / ROT)
    angles = direction * positions[:, None] * frequency[None, :]
    cosine = jnp.cos(angles)[:, None, :]
    sine_part = jnp.sin(angles)[:, None, :]
    first_half = block[..., :half_rot]
    second = block[..., half_rot:ROT]
    return jnp.concatenate(
        [
            first_half * cosine - second * sine_part,
            second * cosine + first_half * sine_part,
            block[..., ROT:],
        ],
        axis=-1,
    )


def gelu_tanh(values):
    return jax.nn.gelu(values, approximate=True)


def gelu_back(expanded, upstream):
    unused_out, pullback = jax.vjp(gelu_tanh, expanded)
    return pullback(upstream)[0]


def heads_of(rows):
    return rows.reshape(rows.shape[0], H, HD)


def scores_of(query_rows, key_rows):
    score_scale = HD ** (-0.5)
    return (
        jnp.einsum(
            "qhd,khd->hqk",
            heads_of(query_rows),
            heads_of(key_rows),
            preferred_element_type=jnp.float32,
        )
        * score_scale
    )


def shards(
    hidden_in,
    out_cotangent,
    norm_gain,
    norm_shift,
    attend_in,
    attend_out,
    expand_weight,
    expand_bias,
    reduce_weight,
    reduce_bias,
    gain_moment,
    shift_moment,
    inward_moment,
    outward_moment,
    expand_moment,
    expbias_moment,
    reduce_moment,
    redbias_moment,
    learn_rate,
    decay_rate,
):
    score_scale = HD ** (-0.5)
    gain_low, shift_low, inward_mat, outward_mat, expand_mat, expand_vec, reduce_mat, reduce_vec = (
        lax.all_gather(norm_gain.astype(jnp.bfloat16), ("dp", "seq"), axis=0, tiled=True),
        lax.all_gather(norm_shift.astype(jnp.bfloat16), ("dp", "seq"), axis=0, tiled=True),
        lax.all_gather(attend_in.astype(jnp.bfloat16), ("dp", "seq"), axis=0, tiled=True),
        lax.all_gather(attend_out.astype(jnp.bfloat16), ("dp", "seq"), axis=0, tiled=True),
        lax.all_gather(expand_weight.astype(jnp.bfloat16), ("dp", "seq"), axis=0, tiled=True),
        lax.all_gather(expand_bias.astype(jnp.bfloat16), ("dp", "seq"), axis=0, tiled=True),
        lax.all_gather(reduce_weight.astype(jnp.bfloat16), ("dp", "seq"), axis=0, tiled=True),
        lax.all_gather(reduce_bias.astype(jnp.bfloat16), ("dp", "seq"), axis=0, tiled=True),
    )
    seq_count, block_len, model_width = hidden_in.shape
    row_count = seq_count * block_len
    full_len = block_len * lax.axis_size("seq")
    seq_start = lax.axis_index("seq") * block_len
    query_index = seq_start + jnp.arange(block_len, dtype=jnp.int32)
    key_index = jnp.arange(full_len, dtype=jnp.int32)
    causal = key_index[None, :] <= query_index[:, None]
    positions = query_index.astype(jnp.float32)
    inputs = hidden_in.astype(jnp.float32).reshape(row_count, model_width)
    row_mean = jnp.mean(inputs, axis=-1, keepdims=True)
    centred = inputs - row_mean
    row_var = jnp.mean(centred * centred, axis=-1, keepdims=True)
    inverse = lax.rsqrt(row_var + epsilon)
    unit_rows = centred * inverse
    gain_full = gain_low.astype(jnp.float32)
    normed = (unit_rows * gain_full + shift_low.astype(jnp.float32)).astype(jnp.bfloat16)
    joined = jnp.dot(normed, inward_mat, preferred_element_type=jnp.float32).reshape(
        seq_count, block_len, 3 * D
    )
    query = (
        rotary(joined[..., :D].reshape(seq_count, block_len, H, HD), positions, 1.0)
        .astype(jnp.bfloat16)
        .reshape(seq_count, block_len, D)
    )
    keyed = (
        rotary(joined[..., D : 2 * D].reshape(seq_count, block_len, H, HD), positions, 1.0)
        .astype(jnp.bfloat16)
        .reshape(seq_count, block_len, D)
    )
    valued = joined[..., 2 * D :].astype(jnp.bfloat16)
    key_all, value_all = (
        lax.all_gather(keyed, "seq", axis=1, tiled=True),
        lax.all_gather(valued, "seq", axis=1, tiled=True),
    )

    def attend(operands):
        query_seq, key_seq, value_seq = operands
        scores = jnp.where(causal[None], scores_of(query_seq, key_seq), masked_score)
        row_max = jnp.max(scores, axis=-1, keepdims=True)
        log_total = row_max + jnp.log(jnp.sum(jnp.exp(scores - row_max), axis=-1, keepdims=True))
        weights = jnp.exp(scores - log_total).astype(jnp.bfloat16)
        mixed = jnp.einsum(
            "hqk,khd->qhd", weights, heads_of(value_seq), preferred_element_type=jnp.float32
        )
        return (mixed.reshape(-1, D).astype(jnp.bfloat16), jnp.transpose(log_total[..., 0]))

    attended, log_totals = lax.map(attend, (query, key_all, value_all))
    expanded = jnp.dot(normed, expand_mat, preferred_element_type=jnp.float32) + expand_vec.astype(
        jnp.float32
    )
    activated = gelu_tanh(expanded).astype(jnp.bfloat16)
    flat_attn = attended.reshape(row_count, D)
    result = (
        inputs
        + jnp.dot(flat_attn, outward_mat, preferred_element_type=jnp.float32)
        + jnp.dot(activated, reduce_mat, preferred_element_type=jnp.float32)
        + reduce_vec.astype(jnp.float32)
    )
    hidden_out = result.astype(jnp.bfloat16).reshape(seq_count, block_len, D)
    upstream = out_cotangent.reshape(row_count, D)
    grad_outward = jnp.einsum("rd,re->de", flat_attn, upstream, preferred_element_type=jnp.float32)
    grad_reduce = jnp.einsum("rf,re->fe", activated, upstream, preferred_element_type=jnp.float32)
    grad_redbias = jnp.sum(upstream.astype(jnp.float32), axis=0)
    attn_back = (
        jnp.einsum("re,de->rd", upstream, outward_mat, preferred_element_type=jnp.float32)
        .astype(jnp.bfloat16)
        .reshape(seq_count, block_len, D)
    )
    act_back = jnp.einsum("re,fe->rf", upstream, reduce_mat, preferred_element_type=jnp.float32)
    expand_back = gelu_back(expanded, act_back).astype(jnp.bfloat16)
    grad_expbias = jnp.sum(expand_back.astype(jnp.float32), axis=0)
    grad_expand = jnp.einsum("rd,rf->df", normed, expand_back, preferred_element_type=jnp.float32)
    norm_back = jnp.einsum("rf,df->rd", expand_back, expand_mat, preferred_element_type=jnp.float32)

    def query_side(query_seq, key_seq, value_seq, back_seq, total_seq):
        scores = jnp.where(causal[None], scores_of(query_seq, key_seq), masked_score)
        probs = jnp.exp(scores - jnp.transpose(total_seq)[:, :, None])
        prob_grad = jnp.einsum(
            "qhd,khd->hqk",
            heads_of(back_seq),
            heads_of(value_seq),
            preferred_element_type=jnp.float32,
        )
        row_delta = jnp.sum(probs * prob_grad, axis=-1, keepdims=True)
        score_grad = (probs * (prob_grad - row_delta)).astype(jnp.bfloat16)
        query_grad = (
            jnp.einsum(
                "hqk,khd->qhd", score_grad, heads_of(key_seq), preferred_element_type=jnp.float32
            )
            * score_scale
        )
        return (probs, score_grad, query_grad, row_delta)

    def attend_back(operands):
        query_seq, key_seq, value_seq, back_seq, total_seq = operands
        probs, score_grad, query_grad, row_delta = query_side(
            query_seq, key_seq, value_seq, back_seq, total_seq
        )
        key_grad = (
            jnp.einsum(
                "hqk,qhd->khd", score_grad, heads_of(query_seq), preferred_element_type=jnp.float32
            )
            * score_scale
        )
        value_grad = jnp.einsum(
            "hqk,qhd->khd",
            probs.astype(jnp.bfloat16),
            heads_of(back_seq),
            preferred_element_type=jnp.float32,
        )
        return (query_grad, key_grad.reshape(-1, D), value_grad.reshape(-1, D))

    query_grads, key_terms, value_terms = lax.map(
        attend_back, (query, key_all, value_all, attn_back, log_totals)
    )
    key_grads, value_grads = (
        lax.psum_scatter(key_terms, "seq", scatter_dimension=1, tiled=True),
        lax.psum_scatter(value_terms, "seq", scatter_dimension=1, tiled=True),
    )
    query_turned = rotary(query_grads, positions, -1.0).reshape(seq_count, block_len, D)
    key_turned = rotary(key_grads.reshape(seq_count, block_len, H, HD), positions, -1.0).reshape(
        seq_count, block_len, D
    )
    joined_back = (
        jnp.concatenate([query_turned, key_turned, value_grads], axis=-1)
        .astype(jnp.bfloat16)
        .reshape(row_count, 3 * D)
    )
    grad_inward = jnp.einsum("rd,re->de", normed, joined_back, preferred_element_type=jnp.float32)
    norm_back = norm_back + jnp.einsum(
        "re,de->rd", joined_back, inward_mat, preferred_element_type=jnp.float32
    )
    grad_gain = jnp.sum(norm_back * unit_rows, axis=0)
    grad_shift = jnp.sum(norm_back, axis=0)
    unit_back = norm_back * gain_full
    input_back = inverse * (
        unit_back
        - jnp.mean(unit_back, axis=-1, keepdims=True)
        - unit_rows * jnp.mean(unit_back * unit_rows, axis=-1, keepdims=True)
    ) + upstream.astype(jnp.float32)
    hidden_grad = input_back.astype(jnp.bfloat16).reshape(seq_count, block_len, D)
    totals = (
        lax.psum_scatter(grad_gain, ("dp", "seq"), scatter_dimension=0, tiled=True),
        lax.psum_scatter(grad_shift, ("dp", "seq"), scatter_dimension=0, tiled=True),
        lax.psum_scatter(grad_inward, ("dp", "seq"), scatter_dimension=0, tiled=True),
        lax.psum_scatter(grad_outward, ("dp", "seq"), scatter_dimension=0, tiled=True),
        lax.psum_scatter(grad_expand, ("dp", "seq"), scatter_dimension=0, tiled=True),
        lax.psum_scatter(grad_expbias, ("dp", "seq"), scatter_dimension=0, tiled=True),
        lax.psum_scatter(grad_reduce, ("dp", "seq"), scatter_dimension=0, tiled=True),
        lax.psum_scatter(grad_redbias, ("dp", "seq"), scatter_dimension=0, tiled=True),
    )
    seq_total = seq_count * lax.axis_size("dp")
    step_rate = learn_rate[0]
    decay_now = decay_rate[0]
    params = (
        norm_gain,
        norm_shift,
        attend_in,
        attend_out,
        expand_weight,
        expand_bias,
        reduce_weight,
        reduce_bias,
    )
    moments = (
        gain_moment,
        shift_moment,
        inward_moment,
        outward_moment,
        expand_moment,
        expbias_moment,
        reduce_moment,
        redbias_moment,
    )
    momenta = [
        0.5 * moment + 0.5 * (summed_grad / seq_total)
        for moment, summed_grad in zip(moments, totals)
    ]
    updated = [
        (1.0 - decay_now) * weight_now - step_rate * momentum
        for weight_now, momentum in zip(params, momenta)
    ]
    return (
        hidden_out,
        hidden_grad,
        momenta[0],
        momenta[1],
        momenta[2],
        momenta[3],
        momenta[4],
        momenta[5],
        momenta[6],
        momenta[7],
        updated[0],
        updated[1],
        updated[2],
        updated[3],
        updated[4],
        updated[5],
        updated[6],
        updated[7],
    )


def solution(mesh):
    placed = (
        P("dp", "seq", None),
        P("dp", "seq", None),
        P(("dp", "seq")),
        P(("dp", "seq")),
        P(("dp", "seq"), None),
        P(("dp", "seq"), None),
        P(("dp", "seq"), None),
        P(("dp", "seq")),
        P(("dp", "seq"), None),
        P(("dp", "seq")),
        P(("dp", "seq")),
        P(("dp", "seq")),
        P(("dp", "seq"), None),
        P(("dp", "seq"), None),
        P(("dp", "seq"), None),
        P(("dp", "seq")),
        P(("dp", "seq"), None),
        P(("dp", "seq")),
        P(),
        P(),
    )
    return jax.shard_map(
        shards,
        mesh=mesh,
        in_specs=placed,
        out_specs=(
            P("dp", "seq", None),
            P("dp", "seq", None),
            P(("dp", "seq")),
            P(("dp", "seq")),
            P(("dp", "seq"), None),
            P(("dp", "seq"), None),
            P(("dp", "seq"), None),
            P(("dp", "seq")),
            P(("dp", "seq"), None),
            P(("dp", "seq")),
            P(("dp", "seq")),
            P(("dp", "seq")),
            P(("dp", "seq"), None),
            P(("dp", "seq"), None),
            P(("dp", "seq"), None),
            P(("dp", "seq")),
            P(("dp", "seq"), None),
            P(("dp", "seq")),
        ),
        check_vma=False,
    )
```

profile of v0, /device:TPU:13, one launch (start us, length us, event | category | flops | bytes accessed | tf_op | source)
XLA Modules:
  0.0 1242.2 jit_solution(16471111655699511063)
XLA Ops:
  7.2 1.7 convert_element_type.124
  11.6 40.1 %all-reduce.8 = (bf16[1024]{0:T(1024)(128)(2,1)S(1)}, bf16[1024]{0:T(1024)(128)(2,1)S(1)}, bf16[1024]{0:T(1024)(128)(2,1)}) all-reduce(bf16[1024]{0:T(1024)(128)(2,1)S(1)} %dynamic-update-slice.1, bf16[1024]{0:T(1024)(128)(2,1)S(1)} %dynamic-update-slice, ...), channel_id=1, replica_groups=mesh['dp'=4,'seq'=8] {'dp','seq'}, use_global_device_ids=true, to_apply=%add.1 | all-reduce | flops 3072 | bytes 12288
  52.9 1.3 fusion.27
  55.1 27.5 %all-gather.8.cloned.1.call-done = bf16[1024,3072]{1,0:T(8,128)(2,1)} async-done(((bf16[32,3072]{1,0:T(8,128)(2,1)}), bf16[1024,3072]{1,0:T(8,128)(2,1)}) %all-gather.8.cloned.1.call-update) | async-done | bytes 6291472 | tf_op jit(solution)/shard_map/all_gather | solution.py:86
  82.6 4.9 convolution_bitcast_fusion
  87.6 1.5 copy-done.5
  91.7 2.1 slice.111
  94.4 32.6 %all-gather.12.cloned.1.call-done = bf16[1,2048,1024]{1,2,0:T(8,128)(2,1)} async-done(((bf16[1,256,1024]{1,2,0:T(8,128)(2,1)}), bf16[1,2048,1024]{1,2,0:T(8,128)(2,1)}) %all-gather.12.cloned.1.call-update) | async-done | bytes 4194320 | tf_op jit(solution)/shard_map/all_gather | solution.py:124
  127.0 16.5 %fusion = (f32[16,256]{1,0:T(8,128)S(1)}, f32[16,256,2048]{2,1,0:T(8,128)}) fusion(pred[256,2048]{1,0:T(8,128)(4,1)S(1)} %iota_compare_fusion, bf16[2048,16,64]{0,2,1:T(8,128)(2,1)} %bitcast.130, bf16[256,16,32]{0,2,1:T(8,128)(2,1)S(1)} %fusion.40, bf16[256,16,16]{0,2,1:T(8,128)(2,1)S(1)} %get-tuple-element.103, bf16[256,16,16]{0,2,1:T(8,128)(2,1)S(1)} %get-tuple-element.102), kind=kOutput, calls=%fused_computation.5 | convolution fusion | flops 1100476416 | bytes 38813696 | tf_op jit(solution)/shard_map/while/body/eval_jaxpr/qhd,khd->hqk/dot_general | solution.py:50
  143.5 15.4 %exponential_reduce_fusion = f32[16,256]{1,0:T(8,128)S(1)} fusion(f32[16,256,2048]{2,1,0:T(8,128)} %get-tuple-element.121, f32[16,256]{1,0:T(8,128)S(1)} %get-tuple-element.120, pred[256,2048]{1,0:T(8,128)(4,1)S(1)} %iota_compare_fusion), kind=kLoop, calls=%fused_computation.3 | loop fusion | flops 33550336 | bytes 34111488 | tf_op jit(solution)/shard_map/while/body/eval_jaxpr/reduce_sum | solution.py:132
  159.0 7.8 all-gather.10.cloned.1.call-done
  166.7 6.5 copy.54
  173.3 16.0 %convolution_convert_fusion = bf16[16,64,256]{2,1,0:T(8,128)(2,1)S(1)} fusion(bf16[2048,16,64]{0,2,1:T(8,128)(2,1)} %bitcast.132, f32[16,256,2048]{2,1,0:T(8,128)} %get-tuple-element.121, f32[16,256]{1,0:T(8,128)S(1)} %log_add_fusion, pred[256,2048]{1,0:T(8,128)(4,1)S(1)} %iota_compare_fusion), kind=kOutput, calls=%fused_computation.35 | convolution fusion | flops 1107558400 | bytes 38813696 | tf_op jit(solution)/shard_map/while/body/eval_jaxpr/hqk,khd->qhd/dot_general | solution.py:134
  190.0 2.7 fusion.33
  195.8 104.6 %reduce-scatter.13.cloned.1.call-done = f32[32,1024]{1,0:T(8,128)} async-done(((f32[1024,1024]{1,0:T(8,128)}), f32[32,1024]{1,0:T(8,128)}) %reduce-scatter.13.cloned.1.call-update) | async-done | bytes 131088 | tf_op jit(solution)/shard_map/reduce_scatter | solution.py:238
  300.4 1.6 multiply_subtract_fusion.3
  302.2 60.4 %all-gather = bf16[32,1,128]{2,1,0:T(2,128)(2,1)S(1)} all-gather(bf16[1,1,128]{2,1,0:T(2,128)(2,1)S(1)} %convert_bitcast_fusion.2), channel_id=1, replica_groups=mesh['dp'=4,'seq'=8] {'dp','seq'}, dimensions={0}, use_global_device_ids=true | all-gather | bytes 8448 | tf_op jit(solution)/shard_map/all_gather | solution.py:89
  362.5 48.3 %all-gather.16.cloned.1.call-done = bf16[1024,4096]{1,0:T(8,128)(2,1)} async-done(((bf16[32,4096]{1,0:T(8,128)(2,1)}), bf16[1024,4096]{1,0:T(8,128)(2,1)}) %all-gather.16.cloned.1.call-update) | async-done | bytes 8388624 | tf_op jit(solution)/shard_map/all_gather | solution.py:88
  410.8 5.8 convolution_add_fusion
  416.7 2.0 copy-done.1
  418.6 8.6 fusion.31
  427.3 40.9 %all-gather.14.cloned.1.call-done = bf16[1024,1024]{1,0:T(8,128)(2,1)} async-done(((bf16[32,1024]{1,0:T(8,128)(2,1)}), bf16[1024,1024]{1,0:T(8,128)(2,1)}) %all-gather.14.cloned.1.call-update) | async-done | bytes 2097168 | tf_op jit(solution)/shard_map/all_gather | solution.py:87
  468.2 2.3 convolution_convert_fusion.1
  470.7 26.5 %multiply_reduce_fusion = (f32[16,256]{1,0:T(8,128)S(1)}, f32[16,256,2048]{2,1,0:T(8,128)}) fusion(f32[16,256,2048]{2,1,0:T(8,128)} %get-tuple-element.121, f32[16,256]{1,0:T(8,128)S(1)} %log_add_fusion, pred[256,2048]{1,0:T(8,128)(4,1)S(1)} %iota_compare_fusion, bf16[256,16,64]{0,2,1:T(8,128)(2,1)S(1)} %bitcast.141, bf16[2048,16,64]{0,2,1:T(8,128)(2,1)} %bitcast.133), kind=kOutput, calls=%fused_computation.1 | convolution fusion | flops 1115680768 | bytes 72384512 | tf_op jit(solution)/shard_map/while/body/eval_jaxpr/qhd,khd->hqk/dot_general | solution.py:170
  497.2 28.7 %multiply_convert_fusion = bf16[16,256,2048]{2,1,0:T(8,128)(2,1)} fusion(f32[16,256,2048]{2,1,0:T(8,128)} %get-tuple-element.123, f32[16,256,2048]{2,1,0:T(8,128)} %get-tuple-element.121, f32[16,256]{1,0:T(8,128)S(1)} %get-tuple-element.122, f32[16,256]{1,0:T(8,128)S(1)} %log_add_fusion, pred[256,2048]{1,0:T(8,128)(4,1)S(1)} %iota_compare_fusion), kind=kLoop, calls=%fused_computation | loop fusion | flops 50331648 | bytes 84443136 | tf_op jit(solution)/shard_map/while/body/eval_jaxpr/convert_element_type | solution.py:177
  526.0 12.3 convolution_multiply_fusion
  538.3 17.1 %fusion.42 = f32[16,64,2048]{2,1,0:T(8,128)} fusion(bf16[256,16,64]{0,2,1:T(8,128)(2,1)S(1)} %bitcast.142, f32[16,256,2048]{2,1,0:T(8,128)} %get-tuple-element.121, f32[16,256]{1,0:T(8,128)S(1)} %log_add_fusion, pred[256,2048]{1,0:T(8,128)(4,1)S(1)} %iota_compare_fusion), kind=kOutput, calls=%fused_computation.88 | convolution fusion | flops 1107296256 | bytes 43008000 | tf_op jit(solution)/shard_map/while/body/eval_jaxpr/hqk,qhd->khd/dot_general | solution.py:197
  555.5 99.0 %reduce-scatter.17.cloned.1.call-done = f32[128,1024]{1,0:T(8,128)} async-done(((f32[4096,1024]{1,0:T(8,128)}), f32[128,1024]{1,0:T(8,128)}) %reduce-scatter.17.cloned.1.call-update) | async-done | bytes 524304 | tf_op jit(solution)/shard_map/reduce_scatter | solution.py:241
  654.5 2.2 multiply_subtract_fusion
  657.0 12.3 fusion.9
  669.4 59.6 %reduce-scatter.7.cloned.1.call-done = f32[1,256,1024]{1,2,0:T(8,128)} async-done(((f32[1,2048,1024]{1,2,0:T(8,128)}), f32[1,256,1024]{1,2,0:T(8,128)}) %reduce-scatter.7.cloned.1.call-update) | async-done | bytes 1048592 | tf_op jit(solution)/shard_map/reduce_scatter | solution.py:209
  731.4 72.7 %reduce-scatter.9.cloned.1.call-done = f32[1,256,1024]{1,2,0:T(8,128)} async-done(((f32[1,2048,1024]{1,2,0:T(8,128)}), f32[1,256,1024]{1,2,0:T(8,128)}) %reduce-scatter.9.cloned.1.call-update) | async-done | bytes 1048592 | tf_op jit(solution)/shard_map/reduce_scatter | solution.py:210
  804.1 1.3 convert_bitcast_fusion.1
  805.4 6.6 fusion.29
  812.1 73.4 %all-gather.18.cloned.1.call-done = bf16[4096,1024]{1,0:T(8,128)(2,1)} async-done(((bf16[128,1024]{1,0:T(8,128)(2,1)}), bf16[4096,1024]{1,0:T(8,128)(2,1)}) %all-gather.18.cloned.1.call-update) | async-done | bytes 8388624 | tf_op jit(solution)/shard_map/all_gather | solution.py:90
  885.5 11.3 convert_reduce_fusion
  896.8 1.3 copy-done.9
  898.1 9.1 fusion.61
  907.9 135.0 %reduce-scatter.11.cloned.1.call-done = f32[32,3072]{1,0:T(8,128)} async-done(((f32[1024,3072]{1,0:T(8,128)}), f32[32,3072]{1,0:T(8,128)}) %reduce-scatter.11.cloned.1.call-update) | async-done | bytes 393232 | tf_op jit(solution)/shard_map/reduce_scatter | solution.py:237
  1042.9 1.9 multiply_subtract_fusion.2
  1044.9 6.4 fusion.71
  1051.4 5.4 fusion.26
  1056.8 1.3 convert_reduce_fusion.1
  1058.1 45.6 %all-reduce.7 = (f32[1024]{0:T(1024)S(1)}, f32[1024]{0:T(1024)S(1)}, f32[4096]{0:T(1024)S(1)}, f32[1024]{0:T(1024)S(1)}) all-reduce(f32[1024]{0:T(1024)S(1)} %get-tuple-element.69, f32[1024]{0:T(1024)S(1)} %get-tuple-element.72, f32[4096]{0:T(1024)S(1)} %get-tuple-element.125, ...), channel_id=4, replica_groups=mesh['dp'=4,'seq'=8] {'dp','seq'}, use_global_device_ids=true, to_apply=%region_10.11.clone | all-reduce | flops 7168 | bytes 57344
  1105.5 7.7 fusion.60
  1113.3 1.6 fusion.20
  1114.8 118.2 %reduce-scatter.15.cloned.1.call-done = f32[32,4096]{1,0:T(8,128)} async-done(((f32[1024,4096]{1,0:T(8,128)}), f32[32,4096]{1,0:T(8,128)}) %reduce-scatter.15.cloned.1.call-update) | async-done | bytes 524304 | tf_op jit(solution)/shard_map/reduce_scatter | solution.py:239
  1233.0 2.1 multiply_subtract_fusion.1
  (126 shorter events, 16.3 us)
Async XLA Ops:
  7.2 75.4 %all-gather.8.cloned.1.call-start = ((), (), s32[]{:S(2)}) async-start(), calls=%async_computation.6 | async-start | bytes 6488064 | tf_op jit(solution)/shard_map/all_gather | solution.py:86
  9.0 118.1 %all-gather.12.cloned.1.call-start = ((), (), s32[]{:S(2)}) async-start(), calls=%async_computation.8 | async-start | bytes 4718592 | tf_op jit(solution)/shard_map/all_gather | solution.py:124
  87.5 1.7 copy-start.5
  90.7 52.8 %copy-start.11 = (bf16[256,16,16]{0,2,1:T(8,128)(2,1)}, bf16[256,16,16]{0,2,1:T(8,128)(2,1)S(1)}, u32[]{:S(2)}) copy-start(bf16[256,16,16]{0,2,1:T(8,128)(2,1)S(1)} %get-tuple-element.103) | copy-start | bytes 393220
  91.6 75.1 %all-gather.10.cloned.1.call-start = ((), (), s32[]{:S(2)}) async-start(), calls=%async_computation.7 | async-start | bytes 4718592 | tf_op jit(solution)/shard_map/all_gather | solution.py:125
  93.8 206.6 %reduce-scatter.13.cloned.1.call-start = ((), (), s32[]{:S(2)}) async-start(), calls=%async_computation.15 | async-start | bytes 4325376 | tf_op jit(solution)/shard_map/reduce_scatter | solution.py:238
  173.3 16.8 %copy-start.2 = (bf16[1,256,1024]{2,1,0:T(8,128)(2,1)S(1)}, bf16[1,256,1024]{2,1,0:T(8,128)(2,1)}, u32[]{:S(2)}) copy-start(bf16[1,256,1024]{2,1,0:T(8,128)(2,1)} %param.21) | copy-start | bytes 1572868
  189.2 0.8 copy-start.3
  192.7 1.0 copy-start.6
  192.7 107.7 %copy-start.17 = (f32[32,1024]{1,0:T(8,128)S(1)}, f32[32,1024]{1,0:T(8,128)}, u32[]{:S(2)}) copy-start(f32[32,1024]{1,0:T(8,128)} %param.25) | copy-start | bytes 393220
  192.7 107.7 %copy-start.18 = (f32[32,1024]{1,0:T(8,128)S(1)}, f32[32,1024]{1,0:T(8,128)}, u32[]{:S(2)}) copy-start(f32[32,1024]{1,0:T(8,128)} %param.33) | copy-start | bytes 393220
  192.7 109.4 %copy-start.22 = (f32[128]{0:T(128)S(1)}, f32[128]{0:T(128)}, u32[]{:S(2)}) copy-start(f32[128]{0:T(128)} %param.27) | copy-start | bytes 1540
  192.7 218.1 %copy-start = (bf16[1,256,1024]{2,1,0:T(8,128)(2,1)S(1)}, bf16[1,256,1024]{2,1,0:T(8,128)(2,1)}, u32[]{:S(2)}) copy-start(bf16[1,256,1024]{2,1,0:T(8,128)(2,1)} %param.20) | copy-start | bytes 1572868
  192.8 218.1 %all-gather.16.cloned.1.call-start = ((), (), s32[]{:S(2)}) async-start(), calls=%async_computation.10 | async-start | bytes 8650752 | tf_op jit(solution)/shard_map/all_gather | solution.py:88
  194.5 273.7 %all-gather.14.cloned.1.call-start = ((), (), s32[]{:S(2)}) async-start(), calls=%async_computation.9 | async-start | bytes 2162688 | tf_op jit(solution)/shard_map/all_gather | solution.py:87
  302.1 352.4 %reduce-scatter.17.cloned.1.call-start = ((), (), s32[]{:S(2)}) async-start(), calls=%async_computation.17 | async-start | bytes 17301504 | tf_op jit(solution)/shard_map/reduce_scatter | solution.py:241
  416.7 2.0 copy-start.1
  427.3 301.7 %reduce-scatter.7.cloned.1.call-start = ((), (), s32[]{:S(2)}) async-start(), calls=%async_computation.12 | async-start | bytes 9437184 | tf_op jit(solution)/shard_map/reduce_scatter | solution.py:209
  497.2 28.7 %copy-start.12 = (bf16[256,16,16]{0,2,1:T(8,128)(2,1)S(1)}, bf16[256,16,16]{0,2,1:T(8,128)(2,1)}, u32[]{:S(2)}) copy-start(bf16[256,16,16]{0,2,1:T(8,128)(2,1)} %copy-done.11) | copy-start | bytes 393220
  538.3 265.8 %reduce-scatter.9.cloned.1.call-start = ((), (), s32[]{:S(2)}) async-start(), calls=%async_computation.13 | async-start | bytes 9437184 | tf_op jit(solution)/shard_map/reduce_scatter | solution.py:210
  555.4 99.1 %copy-start.14 = (f32[128,1024]{1,0:T(8,128)S(1)}, f32[128,1024]{1,0:T(8,128)}, u32[]{:S(2)}) copy-start(f32[128,1024]{1,0:T(8,128)} %param.28) | copy-start | bytes 1572868
  555.4 99.1 %copy-start.15 = (f32[128,1024]{1,0:T(8,128)S(1)}, f32[128,1024]{1,0:T(8,128)}, u32[]{:S(2)}) copy-start(f32[128,1024]{1,0:T(8,128)} %param.36) | copy-start | bytes 1572868
  555.5 330.0 %all-gather.18.cloned.1.call-start = ((), (), s32[]{:S(2)}) async-start(), calls=%async_computation.11 | async-start | bytes 8650752 | tf_op jit(solution)/shard_map/all_gather | solution.py:90
  656.8 73.3 %copy-start.19 = (f32[256,16]{0,1:T(8,128)S(1)}, f32[256,16]{0,1:T(8,128)}, u32[]{:S(2)}) copy-start(f32[256,16]{0,1:T(8,128)} %get-tuple-element.114) | copy-start | bytes 49156
  656.8 73.3 %copy-start.20 = (f32[256,16]{0,1:T(8,128)S(1)}, f32[256,16]{0,1:T(8,128)}, u32[]{:S(2)}) copy-start(f32[256,16]{0,1:T(8,128)} %get-tuple-element.115) | copy-start | bytes 49156
  656.8 386.1 %reduce-scatter.11.cloned.1.call-start = ((), (), s32[]{:S(2)}) async-start(), calls=%async_computation.14 | async-start | bytes 12976128 | tf_op jit(solution)/shard_map/reduce_scatter | solution.py:237
  812.0 421.0 %reduce-scatter.15.cloned.1.call-start = ((), (), s32[]{:S(2)}) async-start(), calls=%async_computation.16 | async-start | bytes 17301504 | tf_op jit(solution)/shard_map/reduce_scatter | solution.py:239
  896.8 1.3 copy-start.9
  907.3 0.7 copy-start.21
  907.3 135.7 %copy-start.10 = (f32[32,3072]{1,0:T(8,128)S(1)}, f32[32,3072]{1,0:T(8,128)}, u32[]{:S(2)}) copy-start(f32[32,3072]{1,0:T(8,128)} %param.24) | copy-start | bytes 1179652
  907.3 135.7 %copy-start.16 = (f32[32,3072]{1,0:T(8,128)S(1)}, f32[32,3072]{1,0:T(8,128)}, u32[]{:S(2)}) copy-start(f32[32,3072]{1,0:T(8,128)} %param.32) | copy-start | bytes 1179652
  1051.3 52.4 %copy-start.23 = (f32[128]{0:T(128)S(1)}, f32[128]{0:T(128)}, u32[]{:S(2)}) copy-start(f32[128]{0:T(128)} %param.27) | copy-start | bytes 1540
  1051.3 52.4 %copy-start.24 = (f32[128]{0:T(128)S(1)}, f32[128]{0:T(128)}, u32[]{:S(2)}) copy-start(f32[128]{0:T(128)} %param.35) | copy-start | bytes 1540
  1051.3 53.0 %copy-start.25 = (f32[32]{0:T(128)S(1)}, f32[32]{0:T(128)}, u32[]{:S(2)}) copy-start(f32[32]{0:T(128)} %param.22) | copy-start | bytes 388
  1051.3 53.0 %copy-start.26 = (f32[32]{0:T(128)S(1)}, f32[32]{0:T(128)}, u32[]{:S(2)}) copy-start(f32[32]{0:T(128)} %param.30) | copy-start | bytes 388
  1051.3 53.6 %copy-start.27 = (f32[32]{0:T(128)S(1)}, f32[32]{0:T(128)}, u32[]{:S(2)}) copy-start(f32[32]{0:T(128)} %param.23) | copy-start | bytes 388
  1051.3 53.6 %copy-start.28 = (f32[32]{0:T(128)S(1)}, f32[32]{0:T(128)}, u32[]{:S(2)}) copy-start(f32[32]{0:T(128)} %param.29) | copy-start | bytes 388
  1051.3 53.6 %copy-start.29 = (f32[32]{0:T(128)S(1)}, f32[32]{0:T(128)}, u32[]{:S(2)}) copy-start(f32[32]{0:T(128)} %param.37) | copy-start | bytes 388
  1051.4 53.6 %copy-start.30 = (f32[32]{0:T(128)S(1)}, f32[32]{0:T(128)}, u32[]{:S(2)}) copy-start(f32[32]{0:T(128)} %param.31) | copy-start | bytes 388
  1105.5 7.7 copy-start.4
  1105.5 7.7 copy-start.8
  1113.2 119.8 %copy-start.7 = (f32[32,4096]{1,0:T(8,128)S(1)}, f32[32,4096]{1,0:T(8,128)}, u32[]{:S(2)}) copy-start(f32[32,4096]{1,0:T(8,128)} %param.26) | copy-start | bytes 1572868
  1113.3 119.8 %copy-start.13 = (f32[32,4096]{1,0:T(8,128)S(1)}, f32[32,4096]{1,0:T(8,128)}, u32[]{:S(2)}) copy-start(f32[32,4096]{1,0:T(8,128)} %param.34) | copy-start | bytes 1572868
Sparse Core Ops, SparseCore 0:
  11.5 71.0 all-gather.7
  91.7 35.2 all-gather.11
  129.5 37.2 all-gather.9
  192.9 107.5 reduce-scatter.12
  303.7 107.0 all-gather.15
  414.1 54.0 all-gather.13
  470.5 183.9 reduce-scatter.16
  658.0 70.9 reduce-scatter.6
  732.9 71.2 reduce-scatter.8
  807.4 78.0 all-gather.17
  891.5 151.3 reduce-scatter.10
  1045.2 187.8 reduce-scatter.14
where the time goes:
time: 1250 us; the launch traced here: 1240 us
  waiting for transfers between devices  820 us (66%)
  matrix products  173 us (14%)
  blocking collectives  146 us (12%)
  other arithmetic  67.7 us (5%)
  local copies, waits for them, and re-layouts  18.6 us (1%)
  between operations  16.2 us (1%)
    reduce_scatter x1, waiting for transfers between devices, shards(): lax.psum_scatter(grad_inward, ('dp', 'seq'), scatter_dimension=0, tiled=T...  135 us
    reduce_scatter x1, waiting for transfers between devices, shards(): lax.psum_scatter(grad_expand, ('dp', 'seq'), scatter_dimension=0, tiled=T...  118 us
    reduce_scatter x1, waiting for transfers between devices, shards(): lax.psum_scatter(grad_outward, ('dp', 'seq'), scatter_dimension=0, tiled=...  105 us
    reduce_scatter x1, waiting for transfers between devices, shards(): lax.psum_scatter(grad_reduce, ('dp', 'seq'), scatter_dimension=0, tiled=T...  99 us
    unnamed x2, blocking collectives  85.7 us
    all_gather x1, waiting for transfers between devices, shards(): lax.all_gather(reduce_weight.astype(jnp.bfloat16), ('dp', 'seq'), axis=0,...  73.4 us
    reduce_scatter x1, waiting for transfers between devices, shards(): lax.psum_scatter(value_terms, 'seq', scatter_dimension=1, tiled=True)  72.7 us
    all_gather x1, blocking collectives, shards(): lax.all_gather(expand_bias.astype(jnp.bfloat16), ('dp', 'seq'), axis=0, t...  60.4 us
  transfers between devices with their start and end apart: 12, of which 12 were waited for; matrix products, arithmetic and copies ran while one was open for 17% of the time, Pallas kernels for 0%

commit v1 on v0

--- a/solution.py
+++ b/solution.py
@@ -1,6 +1,9 @@
 import jax
 import jax.numpy as jnp
+import numpy as np
 from jax import lax
+from jax.experimental import pallas as pl
+from jax.experimental.pallas import tpu as pltpu
 from jax.sharding import PartitionSpec as P
 
 D = 1024
@@ -294,6 +297,948 @@
     )
 
 
+F32 = jnp.float32
+BF16 = jnp.bfloat16
+MESH = pl.DeviceIdType.MESH
+NZ = 4
+NP = 8
+NT = (((1,), (1,)), ((), ()))
+TN = (((0,), (0,)), ((), ()))
+
+
+def dot(a, b):
+    return jnp.dot(a, b, preferred_element_type=F32)
+
+
+def dot_nt(a, b):
+    return lax.dot_general(a, b, NT, preferred_element_type=F32)
+
+
+def dot_tn(a, b):
+    return lax.dot_general(a, b, TN, preferred_element_type=F32)
+
+
+def aligned(value, unit):
+    return pl.multiple_of(value, unit)
+
+
+def gelu_pair(e):
+    square = e * e
+    t = jnp.tanh(e * (GELU_C + (GELU_C * GELU_A) * square))
+    half = 0.5 + 0.5 * t
+    slope = half + (0.5 * e) * (1.0 - t * t) * (GELU_C + (3.0 * GELU_C * GELU_A) * square)
+    return e * half, slope
+
+
+GELU_C = 0.7978845608028654
+GELU_A = 0.044715
+
+
+def block_kernel(rows, *refs):
+    (
+        x_ref, dy_ref, gain_ref, shift_ref, win_ref, wout_ref, wexp_ref, ebias_ref, wred_ref, rbias_ref,
+        mgain_ref, mshift_ref, min_ref, mout_ref, mexp_ref, mebias_ref, mred_ref, mrbias_ref,
+        rate_ref, decay_ref, cosr_ref, sinr_ref, cosb_ref, sinb_ref,
+        hout_ref, hgrad_ref,
+        ngain_ref, nshift_ref, nin_ref, nout_ref, nexp_ref, nebias_ref, nred_ref, nrbias_ref,
+        ugain_ref, ushift_ref, uin_ref, uout_ref, uexp_ref, uebias_ref, ured_ref, urbias_ref,
+        xg, dyg, xn, win, wexp, wred, wout, wz, pin, pexp,
+        q_s, k_s, vx, o_s, do_s, dkt, dvt, dfused, sbuf, mref, acc, dqacc,
+        act_s, de_s, pdn, sib_o, sib_d, r1_o, r2_o, r1_d, r2_d,
+        gin, gexp, gred, gout, gz, rz_in, rz_exp, rz_red, rz_out, ra_in, ra_exp,
+        vt, vecs, geb, sv, rv, zt, rzv,
+        a2a_s, a2a_r, ag_s, ag_r, z_s, z_r, vz_s, vz_r, vp_s, vp_r, wo_s, wo_r,
+        rs_s, rs_r, zr_s, zr_r, go_s, go_r, b_s, b_r, sp_s, sp_r, sz_s, sz_r,
+    ) = refs
+    pout = xg
+    d = lax.axis_index("dp")
+    s = lax.axis_index("seq")
+    core = lax.rem(s, 2)
+    xbit = lax.rem(lax.div(s, 2), 2)
+    ybit = lax.div(s, 4)
+    chip = lax.div(s, 2)
+    quad = lax.rem(s, 4)
+
+    def peer(m):
+        out = s
+        if m & 1:
+            out = out + (1 - 2 * core)
+        if m & 2:
+            out = out + 2 * (1 - 2 * xbit)
+        if m & 4:
+            out = out + 4 * (1 - 2 * ybit)
+        return out
+
+    def pair_of(t):
+        return 2 * lax.rem(t, 4) + lax.div(t, 4)
+
+    def rc(src, dst, ssem, rsem, dd, ss):
+        return pltpu.make_async_remote_copy(
+            src_ref=src, dst_ref=dst, send_sem=ssem, recv_sem=rsem,
+            device_id=(dd, ss), device_id_type=MESH,
+        )
+
+    lanes = lax.broadcasted_iota(jnp.int32, (8, 128), 1)
+    zrow = jnp.zeros((1, 96), F32)
+    small = jnp.concatenate(
+        [
+            jnp.concatenate([r[...].astype(BF16).astype(F32), zrow], axis=1)
+            for r in (gain_ref, shift_ref, rbias_ref)
+        ]
+        + [jnp.zeros((5, 128), F32)],
+        axis=0,
+    )
+    small = pltpu.roll(small, 32 * quad, 1)
+    rows8 = lax.broadcasted_iota(jnp.int32, (8, 128), 0)
+    ebias_row = jnp.broadcast_to(ebias_ref[...].astype(BF16).astype(F32), (8, 128))
+    vt[s, d] = jnp.where(rows8 == 3, ebias_row, small)
+
+    own_rows = aligned(32 * (8 * d + s), 32)
+    for m in range(NP):
+        t = peer(m)
+        j = pair_of(t)
+        for part in range(3):
+            piece = win_ref[:, pl.ds(aligned(128 * j + 1024 * part, 128), 128)].astype(BF16)
+            if m == 0:
+                win[pl.ds(own_rows, 32), 128 * part : 128 * (part + 1)] = piece
+            else:
+                pin[m, :, 128 * part : 128 * (part + 1)] = piece
+        for e in range(NZ):
+            piece = wexp_ref[:, pl.ds(aligned(128 * (8 * e + t), 128), 128)].astype(BF16)
+            if m == 0:
+                wexp[pl.ds(own_rows, 32), 128 * e : 128 * (e + 1)] = piece
+            else:
+                pexp[m, :, 128 * e : 128 * (e + 1)] = piece
+    wz[d] = wout_ref[...].astype(BF16)
+    wred[pl.ds(aligned(128 * d, 128), 128), :] = wred_ref[...].astype(BF16)
+    xg[pl.ds(aligned(rows * s, rows), rows), :] = x_ref[...]
+    dyg[pl.ds(aligned(rows * s, rows), rows), :] = dy_ref[...]
+
+    barrier = pltpu.get_barrier_semaphore()
+    for m in range(1, NP):
+        pl.semaphore_signal(barrier, inc=1, device_id=(d, peer(m)), device_id_type=MESH)
+    for dz in range(1, NZ):
+        pl.semaphore_signal(barrier, inc=1, device_id=(lax.rem(d + dz, NZ), s), device_id_type=MESH)
+    pl.semaphore_wait(barrier, NP - 1 + NZ - 1)
+
+    def a2a_msg(which, m):
+        src = (pin, pexp)[which].at[m]
+        dst = (win, wexp)[which].at[pl.ds(own_rows, 32)]
+        return rc(src, dst, a2a_s.at[which, m], a2a_r.at[which, m], d, peer(m))
+
+    def a2a_arrived(which, m):
+        dst = (win, wexp)[which].at[pl.ds(aligned(32 * (8 * d + peer(m)), 32), 32)]
+        rc((pin, pexp)[which].at[m], dst, a2a_s.at[which, m], a2a_r.at[which, m], d, peer(m)).wait_recv()
+
+    half = rows // 2
+    AG = (
+        (1, 0, 0, rows), (2, 0, 0, rows), (4, 0, 0, rows),
+        (1, 2, 0, rows), (1, 4, 0, rows), (4, 2, half, half), (2, 4, 0, half),
+        (1, 6, 0, half), (1, 6, half, half),
+    )
+
+    def ag_copy(which, i, incoming):
+        to, blk, lo, n = AG[i]
+        buf = (xg, dyg)[which]
+        at = rows * peer(blk ^ (to if incoming else 0)) + lo
+        ref = buf.at[pl.ds(aligned(at, half), n)]
+        return rc(ref, ref, ag_s.at[which, i], ag_r.at[which, i], d, peer(to))
+
+    def ag_start(which, i):
+        ag_copy(which, i, False).start()
+
+    def ag_arrived(which, i):
+        ag_copy(which, i, True).wait_recv()
+
+    ZVIEW = (
+        lambda b: win.at[pl.ds(aligned(256 * b, 256), 256)],
+        lambda b: wexp.at[pl.ds(aligned(256 * b, 256), 256)],
+        lambda b: wred.at[pl.ds(aligned(128 * b, 128), 128)],
+        lambda b: wz.at[b],
+    )
+
+    def z_direct(dest):
+        ok = d != dest
+        if dest == NZ - 1:
+            ok = ok & (d != 0)
+        if dest == 0:
+            ok = ok & (d != NZ - 1)
+        return ok
+
+    def z_send(a):
+        for dest in (3, 0, 2, 1):
+            @pl.when(z_direct(dest))
+            def _():
+                rc(ZVIEW[a](d), ZVIEW[a](d), z_s.at[a, dest], z_r.at[a, d], dest, s).start()
+
+    FWD = ((2, 0, 3), (1, 3, 0))
+
+    def z_wait_block(a, b):
+        rc(ZVIEW[a](b), ZVIEW[a](b), z_s.at[a, 4], z_r.at[a, b], d, s).wait_recv()
+
+    def z_forward(a):
+        for at, blk, dest in FWD:
+            @pl.when(d == at)
+            def _():
+                z_wait_block(a, blk)
+                rc(ZVIEW[a](blk), ZVIEW[a](blk), z_s.at[a, 4], z_r.at[a, blk], dest, s).start()
+
+    def z_arrived(a):
+        for b in range(NZ):
+            need = d != b
+            for at, blk, dest in FWD:
+                if blk == b:
+                    need = need & (d != at)
+
+            @pl.when(need)
+            def _():
+                z_wait_block(a, b)
+
+    def z_sent(a):
+        for dest in range(NZ):
+            @pl.when(z_direct(dest))
+            def _():
+                rc(ZVIEW[a](d), ZVIEW[a](d), z_s.at[a, dest], z_r.at[a, d], dest, s).wait_send()
+        for at, blk, dest in FWD:
+            @pl.when(d == at)
+            def _():
+                rc(ZVIEW[a](blk), ZVIEW[a](blk), z_s.at[a, 4], z_r.at[a, blk], dest, s).wait_send()
+
+    def other(i):
+        return lax.rem(d + i, NZ)
+
+    def vz_copy(i, incoming):
+        b = lax.rem(d + NZ - i, NZ) if incoming else d
+        return rc(vt.at[s, b], vt.at[s, b], vz_s.at[i], vz_r.at[i], other(i), s)
+
+    def vp_copy(m, incoming):
+        b = peer(m) if incoming else s
+        return rc(vt.at[b], vt.at[b], vp_s.at[m], vp_r.at[m], d, peer(m))
+
+    for i in range(1, NZ):
+        vz_copy(i, False).start()
+    for m in range(1, NP):
+        a2a_msg(0, m).start()
+    z_send(3)
+    for i in (1, 2, 0):
+        ag_start(0, i)
+    for m in range(1, NP):
+        a2a_msg(1, m).start()
+
+    for i in range(1, NZ):
+        vz_copy(i, True).wait_recv()
+    for m in range(1, NP):
+        vp_copy(m, False).start()
+    for m in range(1, NP):
+        a2a_arrived(0, m)
+    z_send(0)
+    for m in range(1, NP):
+        a2a_arrived(1, m)
+    z_send(1)
+    z_send(2)
+
+    for m in range(1, NP):
+        vp_copy(m, True).wait_recv()
+    for dd in range(NZ):
+        for yy in range(2):
+            group = 2 * dd + yy
+            total = vt[4 * yy, dd]
+            for jj in range(1, 4):
+                total = total + vt[4 * yy + jj, dd]
+            vecs[:, 128 * group : 128 * (group + 1)] = total
+
+    def unit_of(xb):
+        xf = xb.astype(F32)
+        mu = jnp.mean(xf, axis=1, keepdims=True)
+        cen = xf - mu
+        var = jnp.mean(cen * cen, axis=1, keepdims=True)
+        inv = lax.rsqrt(var + epsilon)
+        return cen * inv, inv
+
+    def norm_block(b):
+        def step(c, carry):
+            at = aligned(rows * b + 64 * c, 64)
+            unit, _ = unit_of(xg[pl.ds(at, 64), :])
+            xn[pl.ds(at, 64), :] = (unit * vecs[0:1, :] + vecs[1:2, :]).astype(BF16)
+            return carry
+        lax.fori_loop(0, rows // 64, step, 0)
+
+    lane_b = lax.broadcasted_iota(jnp.int32, (rows, 128), 1)
+    low_head = lane_b < HD
+    in_head = lax.rem(lane_b, HD)
+    first_rot = in_head < ROT // 2
+    second_rot = (in_head >= ROT // 2) & (in_head < ROT)
+
+    def turn(block, b, sign):
+        cb, sb = cosb_ref[pl.ds(b, 1), :], sinb_ref[pl.ds(b, 1), :]
+        cr, sr = cosr_ref[...], sinr_ref[...]
+        co = cr * cb - sr * sb
+        si = (sr * cb + cr * sb) * sign
+        co = jnp.where(in_head < ROT, co, 1.0)
+        up = pltpu.roll(block, 128 - ROT // 2, 1)
+        down = pltpu.roll(block, ROT // 2, 1)
+        mixed = jnp.where(first_rot, -up, down) * si
+        mixed = jnp.where(in_head < ROT, mixed, 0.0)
+        return block * co + mixed
+
+    ag_arrived(0, 1)
+    ag_start(0, 5)
+    ag_start(0, 3)
+    ag_arrived(0, 2)
+    ag_start(0, 6)
+    ag_start(0, 4)
+    for i in (1, 2, 0):
+        ag_start(1, i)
+    norm_block(s)
+    ag_arrived(0, 0)
+    norm_block(peer(1))
+    norm_block(peer(2))
+    norm_block(peer(4))
+    ag_arrived(0, 6)
+    ag_start(0, 7)
+    ag_arrived(0, 5)
+    ag_start(0, 8)
+    ag_arrived(0, 3)
+    norm_block(peer(3))
+    ag_arrived(0, 4)
+    norm_block(peer(5))
+    norm_block(peer(6))
+    ag_arrived(0, 7)
+    ag_arrived(0, 8)
+    norm_block(peer(7))
+
+    z_forward(3)
+    z_arrived(3)
+
+    def wo_copy(m, incoming):
+        src = wz.at[lax.rem(peer(m), 4)]
+        r = lax.rem(peer(m), 4) if incoming else quad
+        dst = wout.at[pl.ds(aligned(32 * r, 32), 32)]
+        return rc(src, dst, wo_s.at[m], wo_r.at[m], d, peer(m))
+
+    for m in range(1, 4):
+        wo_copy(m, False).start()
+    wout[pl.ds(aligned(32 * quad, 32), 32), :] = wz[quad]
+
+    ag_arrived(1, 1)
+    ag_start(1, 5)
+    ag_start(1, 3)
+    ag_arrived(1, 2)
+    ag_start(1, 6)
+    ag_start(1, 4)
+
+    z_forward(0)
+    z_arrived(0)
+
+    def qkv_step(b, carry):
+        at = aligned(rows * b, rows)
+        joined = dot(xn[pl.ds(at, rows), :], win[...])
+        q_s[pl.ds(at, rows), :] = turn(joined[:, :128], b, 1.0).astype(BF16) * jnp.asarray(HD**-0.5, BF16)
+        k_s[pl.ds(at, rows), :] = turn(joined[:, 128:256], b, 1.0).astype(BF16)
+        vx[pl.ds(at, rows), :128] = joined[:, 256:].astype(BF16)
+        vx[pl.ds(at, rows), 128:] = jnp.ones((rows, 128), BF16)
+        return carry
+
+    lax.fori_loop(0, NP, qkv_step, 0)
+    ag_arrived(1, 6)
+    ag_start(1, 7)
+    ag_arrived(1, 5)
+    ag_start(1, 8)
+    for i in (0, 3, 4, 7, 8):
+        ag_arrived(1, i)
+    for m in range(1, 4):
+        wo_copy(m, True).wait_recv()
+
+    def do_step(b, carry):
+        at = aligned(rows * b, rows)
+        do_s[pl.ds(at, rows), :] = dot_nt(dyg[pl.ds(at, rows), :], wout[...]).astype(BF16)
+        return carry
+
+    lax.fori_loop(0, NP, do_step, 0)
+
+    KB = 2 * rows
+
+    def weights_at(h, j):
+        return pl.ds(aligned(rows * (NP // 2 * h + j), rows), rows)
+
+    dkt[...] = jnp.zeros_like(dkt)
+    dvt[...] = jnp.zeros_like(dvt)
+
+    def attend_step(i, carry):
+        at = aligned(rows * i, rows)
+        count = lax.div(i, 2) + 1
+        qi = q_s[pl.ds(at, rows), :]
+        zero = jnp.zeros_like(qi)
+        qh = (jnp.where(low_head, qi, zero), jnp.where(low_head, zero, qi))
+
+        def fold(v):
+            out = v[:, :128]
+            for c in range(1, KB // 128):
+                out = jnp.maximum(out, v[:, 128 * c : 128 * (c + 1)])
+            return out
+
+        last = count - 1
+        ka = aligned(KB * last, KB)
+        kj = k_s[pl.ds(ka, KB), :]
+        query = at + lax.broadcasted_iota(jnp.int32, (rows, KB), 0)
+        key = ka + lax.broadcasted_iota(jnp.int32, (rows, KB), 1)
+        for h in range(2):
+            sc = jnp.where(key <= query, dot_nt(qh[h], kj), masked_score)
+            sbuf[h, last] = sc
+            mref[h] = fold(sc)
+
+        def scores(j, c2):
+            kk = k_s[pl.ds(aligned(KB * j, KB), KB), :]
+            for h in range(2):
+                sc = dot_nt(qh[h], kk)
+                sbuf[h, j] = sc
+                mref[h] = jnp.maximum(mref[h], fold(sc))
+            return c2
+
+        lax.fori_loop(0, last, scores, 0)
+        top = [jnp.max(mref[h], axis=1, keepdims=True) for h in range(2)]
+        for h in range(2):
+            mref[h] = jnp.broadcast_to(top[h], (rows, 128))
+            acc[h] = jnp.zeros((rows, 256), F32)
+
+        def weigh(j, c2):
+            vj = vx[pl.ds(aligned(KB * j, KB), KB), :]
+            for h in range(2):
+                pj = jnp.exp(sbuf[h, j] - mref[h][:, :1]).astype(BF16)
+                act_s[weights_at(h, j), :] = pj
+                acc[h] = acc[h] + dot(pj, vj)
+            return c2
+
+        lax.fori_loop(0, count, weigh, 0)
+        recip = [1.0 / acc[h][:, 128:] for h in range(2)]
+        scale = jnp.where(low_head, recip[0], recip[1])
+        of = jnp.where(low_head, acc[0][:, :128], acc[1][:, :128]) * scale
+        o_s[pl.ds(at, rows), :] = of.astype(BF16)
+        doi = do_s[pl.ds(at, rows), :]
+        dof = doi.astype(F32)
+        prod = dof * of
+        delta = (
+            jnp.sum(jnp.where(low_head, prod, 0.0), axis=1, keepdims=True),
+            jnp.sum(jnp.where(low_head, 0.0, prod), axis=1, keepdims=True),
+        )
+        for h in range(2):
+            mref[h] = jnp.broadcast_to(delta[h], (rows, 128))
+            dqacc[h] = jnp.zeros((rows, 128), F32)
+        doh = (jnp.where(low_head, doi, zero), jnp.where(low_head, zero, doi))
+        dot_t = jnp.transpose(dof * scale).astype(BF16)
+        qt = jnp.transpose(qi.astype(F32) * scale).astype(BF16)
+
+        def back(j, c2):
+            ja = aligned(KB * j, KB)
+            kk = k_s[pl.ds(ja, KB), :]
+            vj = vx[pl.ds(ja, KB), :128]
+            for h in range(2):
+                hs = slice(HD * h, HD * (h + 1))
+                pj = act_s[weights_at(h, j), :]
+                dp = dot_nt(doh[h], vj)
+                ds = (pj.astype(F32) * (dp - mref[h][:, :1])).astype(BF16)
+                dqacc[h] = dqacc[h] + dot(ds, kk)
+                dkt[hs, pl.ds(ja, KB)] = dkt[hs, pl.ds(ja, KB)] + dot(qt[hs, :], ds)
+                dvt[hs, pl.ds(ja, KB)] = dvt[hs, pl.ds(ja, KB)] + dot(dot_t[hs, :], pj)
+            return c2
+
+        lax.fori_loop(0, count, back, 0)
+        dq = jnp.where(low_head, dqacc[0], dqacc[1]) * (scale * HD**-0.5)
+        dfused[pl.ds(at, rows), :128] = turn(dq, i, -1.0).astype(BF16)
+
+        @pl.when(i == 3)
+        def _():
+            z_forward(1)
+
+        @pl.when(i == 6)
+        def _():
+            z_forward(2)
+        return carry
+
+    lax.fori_loop(0, NP, attend_step, 0)
+
+    def kv_step(b, carry):
+        at = aligned(rows * b, rows)
+        dk = jnp.transpose(dkt[:, pl.ds(at, rows)])
+        dv = jnp.transpose(dvt[:, pl.ds(at, rows)])
+        dfused[pl.ds(at, rows), 128:256] = turn(dk, b, -1.0).astype(BF16)
+        dfused[pl.ds(at, rows), 256:] = dv.astype(BF16)
+        return carry
+
+    lax.fori_loop(0, NP, kv_step, 0)
+
+    GVIEW = (
+        lambda b: gin.at[pl.ds(aligned(256 * b, 256), 256)],
+        lambda b: gexp.at[pl.ds(aligned(256 * b, 256), 256)],
+        lambda b: gred.at[pl.ds(aligned(128 * b, 128), 128)],
+        lambda b: gz.at[b],
+    )
+    RZ = (rz_in, rz_exp, rz_red, rz_out)
+    COMB = ((0, 1, 3), (3, 2, 0))
+
+    def zr_direct(dest):
+        ok = d != dest
+        if dest == 3:
+            ok = ok & (d != 0) & (d != 1)
+        if dest == 0:
+            ok = ok & (d != 3) & (d != 2)
+        return ok
+
+    def zr_copy(a, src_block, dest, slot, sem):
+        return rc(GVIEW[a](src_block), RZ[a].at[slot], zr_s.at[a, sem], zr_r.at[a, slot], dest, s)
+
+    def zr_first(a):
+        for src, via, dest in COMB:
+            @pl.when(d == src)
+            def _():
+                zr_copy(a, dest, via, via, dest).start()
+
+    def zr_send(a):
+        for dest in (3, 0, 2, 1):
+            @pl.when(zr_direct(dest))
+            def _():
+                zr_copy(a, dest, dest, d, dest).start()
+
+    def zr_join(a):
+        for src, via, dest in COMB:
+            @pl.when(d == via)
+            def _():
+                zr_copy(a, dest, dest, d, dest).wait_recv()
+                ref = GVIEW[a](dest)
+                ref[...] = (ref[...].astype(F32) + RZ[a][via].astype(F32)).astype(BF16)
+                zr_copy(a, dest, dest, d, dest).start()
+
+    def zr_total(a):
+        ref = GVIEW[a](d)
+        for src in range(NZ):
+            came = d != src
+            if src == 0:
+                came = came & (d != 3)
+            if src == 3:
+                came = came & (d != 0)
+
+            @pl.when(came)
+            def _():
+                zr_copy(a, d, d, src, src).wait_recv()
+        use = []
+        for src in range(NZ):
+            came = d != src
+            if src == 0:
+                came = came & (d != 3)
+            if src == 3:
+                came = came & (d != 0)
+            use.append(came)
+        return ref, use
+
+    def zr_sum(a, use, base, at, n):
+        total = base
+        for src in range(NZ):
+            piece = RZ[a][src, pl.ds(at, n), :].astype(F32)
+            total = total + jnp.where(use[src], piece, 0.0)
+        return total
+
+    def zr_sent(a):
+        for dest in range(NZ):
+            sent = d != dest
+
+            @pl.when(sent)
+            def _():
+                zr_copy(a, dest, dest, d, dest).wait_send()
+
+    def gin_block(b):
+        at = aligned(256 * b, 256)
+        gin[pl.ds(at, 256), :] = dot_tn(xn[:, pl.ds(at, 256)], dfused[...]).astype(BF16)
+
+    def gexp_block(b):
+        at = aligned(256 * b, 256)
+        gexp[pl.ds(at, 256), :] = dot_tn(xn[:, pl.ds(at, 256)], de_s[...]).astype(BF16)
+
+    def gred_block(b):
+        at = aligned(128 * b, 128)
+        gred[pl.ds(at, 128), :] = dot_tn(act_s[:, pl.ds(at, 128)], dyg[...]).astype(BF16)
+
+    def loop(n, f):
+        def step(i, carry):
+            f(i)
+            return carry
+        lax.fori_loop(0, n, step, 0)
+
+    loop(NZ, gin_block)
+    zr_first(0)
+    zr_send(0)
+    gout[...] = dot_tn(o_s[...], dyg[...]).astype(BF16)
+
+    def go_copy(m, incoming):
+        t4 = lax.rem(peer(m), 4)
+        src = gout.at[pl.ds(aligned(32 * t4, 32), 32)]
+        dst = gz.at[t4 if incoming else quad]
+        return rc(src, dst, go_s.at[m], go_r.at[m], d, peer(m))
+
+    for m in range(1, 4):
+        go_copy(m, False).start()
+    gz[quad] = gout[pl.ds(aligned(32 * quad, 32), 32), :]
+
+    z_arrived(1)
+    z_arrived(2)
+    eb = jnp.concatenate([vt[s, dd, 3:4, :] for dd in range(NZ)], axis=1)
+    geb[...] = jnp.zeros_like(geb)
+
+    def ffn_block(b):
+        at = aligned(rows * b, rows)
+        e = dot(xn[pl.ds(at, rows), :], wexp[...]) + eb
+        up = dot_nt(dyg[pl.ds(at, rows), :], wred[...])
+        a, slope = gelu_pair(e)
+        act_s[pl.ds(at, rows), :] = a.astype(BF16)
+        de = (up * slope).astype(BF16)
+        de_s[pl.ds(at, rows), :] = de
+        geb[...] = geb[...] + jnp.sum(de.astype(F32).reshape(rows // 8, 8, 4 * 128), axis=0)
+
+    loop(NP, ffn_block)
+    for m in range(1, 4):
+        go_copy(m, True).wait_recv()
+    zr_first(3)
+    zr_send(3)
+    zr_join(0)
+    loop(NZ, gred_block)
+    zr_first(2)
+    zr_send(2)
+    zr_join(3)
+    loop(NZ, gexp_block)
+    zr_first(1)
+    zr_send(1)
+    zr_join(2)
+
+    for i in range(9):
+        ag_copy(0, i, False).wait_send()
+
+    def out_block(b):
+        at = aligned(rows * b, rows)
+        pout[pl.ds(at, rows), :] = (
+            dot(o_s[pl.ds(at, rows), :], wout[...]) + dot(act_s[pl.ds(at, rows), :], wred[...])
+        ).astype(BF16)
+
+    def dn_block(b):
+        at = aligned(rows * b, rows)
+        pdn[pl.ds(at, rows), :] = (
+            dot_nt(de_s[pl.ds(at, rows), :], wexp[...]) + dot_nt(dfused[pl.ds(at, rows), :], win[...])
+        ).astype(BF16)
+
+    RS = ((pout, sib_o, r1_o, r2_o), (pdn, sib_d, r1_d, r2_d))
+
+    def part(which, m, lo, n):
+        return RS[which][0].at[pl.ds(aligned(rows * peer(m) + lo, half), n)]
+
+    RSM = (
+        (1, 7, 0, rows, lambda w: RS[w][1].at[0]),
+        (1, 3, 0, rows, lambda w: RS[w][1].at[1]),
+        (1, 5, 0, rows, lambda w: RS[w][1].at[2]),
+        (1, 1, 0, rows, lambda w: RS[w][1].at[3]),
+        (2, 6, 0, half, lambda w: RS[w][2].at[0]),
+        (4, 6, half, half, lambda w: RS[w][2].at[1]),
+        (2, 2, 0, rows, lambda w: RS[w][3].at[0]),
+        (4, 4, 0, rows, lambda w: RS[w][3].at[1]),
+    )
+
+    def rs_copy(w, i):
+        to, blk, lo, n, land = RSM[i]
+        return rc(part(w, blk, lo, n), land(w), rs_s.at[w, i], rs_r.at[w, i], d, peer(to))
+
+    def add_into(w, m, lo, n, came):
+        def step(c):
+            ref = RS[w][0].at[pl.ds(aligned(rows * peer(m) + lo + 64 * c, 64), 64)]
+            ref[...] = (ref[...].astype(F32) + came[pl.ds(aligned(64 * c, 64), 64), :].astype(F32)).astype(BF16)
+        loop(n // 64, step)
+
+    def rs_one(w):
+        rs_copy(w, 0).wait_recv()
+        add_into(w, 6, 0, rows, RS[w][1].at[0])
+        rs_copy(w, 4).start()
+        rs_copy(w, 5).start()
+        rs_copy(w, 1).wait_recv()
+        add_into(w, 2, 0, rows, RS[w][1].at[1])
+        rs_copy(w, 2).wait_recv()
+        add_into(w, 4, 0, rows, RS[w][1].at[2])
+
+    def rs_two(w):
+        rs_copy(w, 5).wait_recv()
+        add_into(w, 2, half, half, RS[w][2].at[1])
+        rs_copy(w, 6).start()
+        rs_copy(w, 4).wait_recv()
+        add_into(w, 4, 0, half, RS[w][2].at[0])
+        rs_copy(w, 7).start()
+        rs_copy(w, 3).wait_recv()
+
+    def rs_three(w):
+        rs_copy(w, 6).wait_recv()
+        rs_copy(w, 7).wait_recv()
+
+    def rs_total(w, c):
+        at = aligned(64 * c, 64)
+        own = RS[w][0][pl.ds(aligned(rows * s + 64 * c, 64), 64), :].astype(F32)
+        own = own + RS[w][1][3, pl.ds(at, 64), :].astype(F32)
+        own = own + RS[w][3][0, pl.ds(at, 64), :].astype(F32)
+        return own + RS[w][3][1, pl.ds(at, 64), :].astype(F32)
+
+    for i, m in enumerate((7, 3, 5, 1)):
+        out_block(peer(m))
+        rs_copy(0, i).start()
+    for m in (6, 2, 4, 0):
+        out_block(peer(m))
+    zr_join(1)
+    rs_one(0)
+    for i, m in enumerate((7, 3, 5, 1)):
+        dn_block(peer(m))
+        rs_copy(1, i).start()
+    rs_two(0)
+    for m in (6, 2, 4, 0):
+        dn_block(peer(m))
+    rs_one(1)
+    rs_three(0)
+
+    def out_final(c):
+        at = aligned(64 * c, 64)
+        hout_ref[pl.ds(at, 64), :] = (
+            x_ref[pl.ds(at, 64), :].astype(F32) + rs_total(0, c) + vecs[2:3, :]
+        ).astype(BF16)
+
+    loop(rows // 64, out_final)
+    rs_two(1)
+
+    keep = 1.0 - decay_ref[0]
+    rate = rate_ref[0]
+    inv_count = 0.5 / NZ
+
+    def update(w_ref, m_ref, n_ref, u_ref, index, grad):
+        mom = 0.5 * m_ref[index] + grad * inv_count
+        n_ref[index] = mom
+        u_ref[index] = keep * w_ref[index] - rate * mom
+
+    def total_rows(a, n, width):
+        ref, use = zr_total(a)
+
+        def step(c):
+            at = aligned(32 * c, 32)
+            block = ref.at[pl.ds(at, 32)]
+            block[...] = zr_sum(a, use, block[...].astype(F32), at, 32).astype(BF16)
+        loop(n // 32, step)
+
+    def back_copy(which, m, incoming):
+        src = (gin, gexp)[which].at[pl.ds(aligned(256 * d + 32 * peer(m), 32), 32)]
+        dst = (ra_in, ra_exp)[which].at[m]
+        return rc(src, dst, b_s.at[which, m], b_r.at[which, m], d, peer(m))
+
+    total_rows(0, 256, 384)
+    for m in range(1, NP):
+        back_copy(0, m, False).start()
+
+    ref_o, use_o = zr_total(3)
+    update(wout_ref, mout_ref, nout_ref, uout_ref, ..., zr_sum(3, use_o, ref_o[...].astype(F32), 0, 32))
+
+    rs_three(1)
+    sv0 = jnp.zeros((8, 1024), F32)
+    geb_row = jnp.sum(geb[...], axis=0, keepdims=True)
+
+    def grad_final(c, carry):
+        at = aligned(32 * c, 32)
+        dn = rs_total32(1, c)
+        unit, inv = unit_of(x_ref[pl.ds(at, 32), :])
+        dyf = dy_ref[pl.ds(at, 32), :].astype(F32)
+        g = dn * vecs[0:1, :]
+        hg = inv * (
+            g - jnp.mean(g, axis=1, keepdims=True) - unit * jnp.mean(g * unit, axis=1, keepdims=True)
+        ) + dyf
+        hgrad_ref[pl.ds(at, 32), :] = hg.astype(BF16)
+
+        def fold8(v):
+            out = v[0:8]
+            for r in range(8, 32, 8):
+                out = out + v[r : r + 8]
+            return out
+        return (carry[0] + fold8(dn * unit), carry[1] + fold8(dn), carry[2] + fold8(dyf))
+
+    def rs_total32(w, c):
+        at = aligned(32 * c, 32)
+        own = RS[w][0][pl.ds(aligned(rows * s + 32 * c, 32), 32), :].astype(F32)
+        own = own + RS[w][1][3, pl.ds(at, 32), :].astype(F32)
+        own = own + RS[w][3][0, pl.ds(at, 32), :].astype(F32)
+        return own + RS[w][3][1, pl.ds(at, 32), :].astype(F32)
+
+    sums = lax.fori_loop(0, rows // 32, grad_final, (sv0, sv0, sv0))
+    row_sums = [jnp.sum(v, axis=0, keepdims=True) for v in sums]
+    stacked = jnp.concatenate(row_sums + [jnp.zeros((5, 1024), F32)], axis=0)
+    for yy in range(2):
+        for dd in range(NZ):
+            group = 2 * dd + yy
+            sv[yy, dd] = stacked[:, 128 * group : 128 * (group + 1)]
+
+    def sp_copy(m):
+        return rc(sv.at[lax.div(peer(m), 4)], rv.at[m], sp_s.at[m], sp_r.at[m], d, peer(m))
+
+    for m in range(1, NP):
+        sp_copy(m).start()
+
+    ref_r, use_r = zr_total(2)
+
+    def red_update(c):
+        at = aligned(16 * c, 16)
+        update(
+            wred_ref, mred_ref, nred_ref, ured_ref, (pl.ds(at, 16), slice(None)),
+            zr_sum(2, use_r, ref_r[pl.ds(at, 16), :].astype(F32), at, 16),
+        )
+    loop(8, red_update)
+    for m in range(1, NP):
+        sp_copy(m).wait_recv()
+    tiles = sv[ybit]
+    for m in range(1, NP):
+        tiles = tiles + rv[m]
+    for dd in range(NZ):
+        ebt = jnp.broadcast_to(geb_row[:, 128 * dd : 128 * (dd + 1)], (8, 128))
+        zt[dd] = jnp.where(rows8 == 3, ebt, tiles[dd])
+
+    def sz_copy(i, incoming):
+        return rc(zt.at[other(i)], rzv.at[i], sz_s.at[i], sz_r.at[i], other(i), s)
+
+    for i in range(1, NZ):
+        sz_copy(i, False).start()
+
+    total_rows(1, 256, 512)
+    for m in range(1, NP):
+        back_copy(1, m, False).start()
+
+    def strip_in(m, grads):
+        j = pair_of(peer(m))
+        for prt in range(3):
+            cols = pl.ds(aligned(128 * j + 1024 * prt, 128), 128)
+            update(win_ref, min_ref, nin_ref, uin_ref, (slice(None), cols), grads[:, 128 * prt : 128 * (prt + 1)])
+
+    def strip_exp(m, grads):
+        t = peer(m)
+        for e in range(NZ):
+            cols = pl.ds(aligned(128 * (8 * e + t), 128), 128)
+            update(wexp_ref, mexp_ref, nexp_ref, uexp_ref, (slice(None), cols), grads[:, 128 * e : 128 * (e + 1)])
+
+    mine = pl.ds(aligned(256 * d + 32 * s, 32), 32)
+    strip_in(0, gin[mine, :].astype(F32))
+    for m in range(1, NP):
+        back_copy(0, m, True).wait_recv()
+        strip_in(m, ra_in[m].astype(F32))
+
+    for i in range(1, NZ):
+        sz_copy(i, True).wait_recv()
+    tile = zt[d]
+    for i in range(1, NZ):
+        tile = tile + rzv[i]
+    update(ebias_ref, mebias_ref, nebias_ref, uebias_ref, ..., tile[3:4, :])
+    tile = pltpu.roll(tile, lax.rem(128 - 32 * quad, 128), 1)
+    for r, (w, mo, n, u) in enumerate(
+        (
+            (gain_ref, mgain_ref, ngain_ref, ugain_ref),
+            (shift_ref, mshift_ref, nshift_ref, ushift_ref),
+            (rbias_ref, mrbias_ref, nrbias_ref, urbias_ref),
+        )
+    ):
+        update(w, mo, n, u, ..., tile[r : r + 1, :32])
+
+    strip_exp(0, gexp[mine, :].astype(F32))
+    for m in range(1, NP):
+        back_copy(1, m, True).wait_recv()
+        strip_exp(m, ra_exp[m].astype(F32))
+
+    for m in range(1, NP):
+        a2a_msg(0, m).wait_send()
+        a2a_msg(1, m).wait_send()
+        vp_copy(m, False).wait_send()
+        back_copy(0, m, False).wait_send()
+        back_copy(1, m, False).wait_send()
+        sp_copy(m).wait_send()
+    for m in range(1, 4):
+        wo_copy(m, False).wait_send()
+        go_copy(m, False).wait_send()
+    for i in range(1, NZ):
+        vz_copy(i, False).wait_send()
+        sz_copy(i, False).wait_send()
+    for i in range(9):
+        ag_copy(1, i, False).wait_send()
+    for w in range(2):
+        for i in range(8):
+            rs_copy(w, i).wait_send()
+    for a in range(4):
+        z_sent(a)
+        zr_sent(a)
+
+
+def fused_shards(*args):
+    (hidden_in, out_cotangent), weights, moments = args[:2], args[2:10], args[10:18]
+    rows = hidden_in.shape[1]
+    seq = rows * NP
+    freq = 10000.0 ** (-2.0 * np.arange(ROT // 2) / ROT)
+    lane_freq = np.tile(freq, 128 // (ROT // 2))[None, :]
+    near = np.arange(rows)[:, None] * lane_freq
+    far = (rows * np.arange(NP))[:, None] * lane_freq
+    tables = [jnp.asarray(f(a), F32) for a in (near, far) for f in (np.cos, np.sin)]
+
+    def flat(v):
+        return v.reshape(1, -1) if v.ndim == 1 else v
+
+    shards_in = [flat(w) for w in weights]
+    ff = weights[6].shape[0] * NZ
+    shard_shapes = [jax.ShapeDtypeStruct(w.shape, F32) for w in shards_in]
+    vm = pltpu.VMEM
+    dma = pltpu.SemaphoreType.DMA
+    scratch = [
+        vm((seq, D), BF16), vm((seq, D), BF16), vm((seq, D), BF16),
+        vm((D, 384), BF16), vm((D, ff), BF16), vm((ff, D), BF16), vm((128, D), BF16), vm((NZ, 32, D), BF16),
+        vm((NP, 32, 384), BF16), vm((NP, 32, ff), BF16),
+        vm((seq, 128), BF16), vm((seq, 128), BF16), vm((seq, 256), BF16), vm((seq, 128), BF16), vm((seq, 128), BF16),
+        vm((128, seq), F32), vm((128, seq), F32), vm((seq, 384), BF16),
+        vm((2, NP // 2, rows, 2 * rows), F32),
+        vm((2, rows, 128), F32), vm((2, rows, 256), F32), vm((2, rows, 128), F32),
+        vm((seq, ff), BF16), vm((seq, ff), BF16), vm((seq, D), BF16),
+        vm((4, rows, D), BF16), vm((4, rows, D), BF16),
+        vm((2, rows // 2, D), BF16), vm((2, rows, D), BF16), vm((2, rows // 2, D), BF16), vm((2, rows, D), BF16),
+        vm((D, 384), BF16), vm((D, ff), BF16), vm((ff, D), BF16), vm((128, D), BF16), vm((NZ, 32, D), BF16),
+        vm((NZ, 256, 384), BF16), vm((NZ, 256, ff), BF16), vm((NZ, 128, D), BF16), vm((NZ, 32, D), BF16),
+        vm((NP, 32, 384), BF16), vm((NP, 32, ff), BF16),
+        vm((NP, NZ, 8, 128), F32), vm((8, D), F32), vm((8, ff), F32),
+        vm((2, NZ, 8, 128), F32), vm((NP, NZ, 8, 128), F32), vm((NZ, 8, 128), F32), vm((NZ, 8, 128), F32),
+        dma((2, NP)), dma((2, NP)), dma((2, 9)), dma((2, 9)), dma((4, 5)), dma((4, 4)),
+        dma((NZ,)), dma((NZ,)), dma((NP,)), dma((NP,)), dma((4,)), dma((4,)),
+        dma((2, 8)), dma((2, 8)), dma((4, 4)), dma((4, 4)), dma((4,)), dma((4,)),
+        dma((2, NP)), dma((2, NP)), dma((NP,)), dma((NP,)), dma((NZ,)), dma((NZ,)),
+    ]
+    in_vmem = pl.BlockSpec(memory_space=pltpu.VMEM)
+    in_smem = pl.BlockSpec(memory_space=pltpu.SMEM)
+
+    def body(*refs):
+        block_kernel(rows, *refs)
+
+    rows_shape = jax.ShapeDtypeStruct((rows, D), BF16)
+    outs = pl.pallas_call(
+        body,
+        out_shape=[rows_shape, rows_shape] + shard_shapes + shard_shapes,
+        in_specs=[in_vmem] * 18 + [in_smem] * 2 + [in_vmem] * 4,
+        out_specs=[in_vmem] * 18,
+        scratch_shapes=scratch,
+        compiler_params=pltpu.CompilerParams(
+            collective_id=0, has_side_effects=True, vmem_limit_bytes=63 * 2**20
+        ),
+        name="block_step",
+    )(
+        hidden_in.reshape(rows, D), out_cotangent.reshape(rows, D), *shards_in,
+        *[flat(m) for m in moments], args[18], args[19], tables[0], tables[1], tables[2], tables[3],
+    )
+    small = [w.shape for w in weights]
+    return (
+        outs[0].reshape(hidden_in.shape),
+        outs[1].reshape(hidden_in.shape),
+        *[o.reshape(sh) for o, sh in zip(outs[2:], small + small)],
+    )
+
+
+def fits(mesh):
+    return mesh.shape["dp"] == NZ and mesh.shape["seq"] == NP
+
+
 def solution(mesh):
     placed = (
         P("dp", "seq", None),
@@ -318,7 +1263,7 @@
         P(),
     )
     return jax.shard_map(
-        shards,
+        fused_shards if fits(mesh) else shards,
         mesh=mesh,
         in_specs=placed,
         out_specs=(

time: 1250 us -> 213 us (0.17)
  waiting for transfers between devices: 820 us -> 0 us
  Pallas kernels: 0 us -> 195 us
  matrix products: 173 us -> 0 us
  blocking collectives: 146 us -> 0 us
  other arithmetic: 67.7 us -> 0 us
  between operations: 16.2 us -> 2 us
    reduce_scatter x6 -> x0, waiting for transfers between devices: 589 us -> none  [the longest x1 135 us: shards(): lax.psum_scatter(grad_inward, ('dp', 'seq'), scatter_dimension=0, tiled=T...]
    all_gather x6 -> x0, waiting for transfers between devices: 230 us -> none  [the longest x1 73.4 us: shards(): lax.all_gather(reduce_weight.astype(jnp.bfloat16), ('dp', 'seq'), axis=0,...]
    pallas_call x0 -> x1, Pallas kernels: none -> 195 us  [fused_shards(): pl.pallas_call(body, out_shape=[rows_shape, rows_shape] + shard_shapes +...]
    dot_general x18 -> x0, matrix products: 173 us -> none  [the longest x1 26.5 us: query_side(): jnp.einsum('qhd,khd->hqk', heads_of(back_seq), heads_of(value_seq), prefe...]
    unnamed x2 -> x0, blocking collectives: 85.7 us -> none
    all_gather x1 -> x0, blocking collectives: 60.4 us -> none  [shards(): lax.all_gather(expand_bias.astype(jnp.bfloat16), ('dp', 'seq'), axis=0, t...]
    convert_element_type x11 -> x0, other arithmetic: 33.2 us -> none  [the longest x1 28.7 us: query_side(): score_grad = (probs * (prob_grad - row_delta)).astype(jnp.bfloat16)]
    reduce_sum x4 -> x0, other arithmetic: 19.3 us -> none  [the longest x1 15.4 us: attend(): jnp.sum(jnp.exp(scores - row_max), axis=-1, keepdims=True)]
  transfers between devices with their start and end apart: 12 -> 0, of which waited for: 12 -> 0; matrix products, arithmetic and copies ran while one was open for 17% -> 0% of each run, Pallas kernels for 0% -> 0%
where the time goes in v1:
time: 213 us; the launch traced here: 211 us
  Pallas kernels  195 us (92%)
  local copies, waits for them, and re-layouts  13.8 us (6%)
    pallas_call x1, Pallas kernels, fused_shards(): pl.pallas_call(body, out_shape=[rows_shape, rows_shape] + shard_shapes +...  195 us
    unnamed x52, local copies, waits for them, and re-layouts  13.8 us

profile of v1, /device:TPU:13, one launch (start us, length us, event | category | flops | bytes accessed | tf_op | source)
XLA Modules:
  0.0 211.2 jit_solution(14935800813681952540)
XLA Ops:
  2.0 195.5 %block_step.1 = (bf16[256,1024]{1,0:T(8,128)(2,1)}, bf16[256,1024]{1,0:T(8,128)(2,1)}, f32[1,32]{1,0:T(1,128)}, f32[1,32]{1,0:T(1,128)}, f32[32,3072]{1,0:T(8,12...) custom-call(bf16[256,1024]{1,0:T(8,128)(2,1)} %bitcast.22, ...), custom_call_target="tpu_custom_call" | custom-call | tf_op jit(solution)/shard_map/block_step/pallas_call | solution.py:1216
  197.4 0.0 copy-start.4
  197.4 1.9 copy.62
  199.4 0.0 copy-done.4
  199.4 0.0 copy-start.16
  199.4 0.0 copy-start.6
  199.4 0.8 copy.63
  200.2 0.0 copy-done.16
  200.2 0.0 copy-start.15
  200.2 0.5 copy.64
  200.7 0.1 copy-done.15
  200.8 0.5 copy.65
  201.3 0.0 copy-done.6
  201.3 0.0 copy-start.8
  201.3 0.0 copy-start.3
  201.3 0.7 copy.66
  202.0 0.2 copy-done.8
  202.3 0.7 copy.67
  202.9 0.0 copy-done.3
  202.9 0.0 copy-start.14
  202.9 0.0 copy-start.2
  202.9 0.8 copy.68
  203.7 0.0 copy-done.14
  203.7 0.5 copy.69
  204.3 0.0 copy-done.2
  204.3 0.0 copy-start.5
  204.3 0.8 copy.70
  205.1 0.0 copy-done.13
  205.1 0.0 copy-start.12
  205.1 0.5 copy.71
  205.6 0.1 copy-done.12
  205.7 0.0 copy-start.11
  205.7 0.5 copy.72
  206.2 0.2 copy-done.11
  206.4 0.5 copy.73
  206.9 0.0 copy-done.5
  206.9 0.0 copy-start.7
  206.9 0.7 copy.74
  207.7 0.2 copy-done.7
  207.9 0.7 copy.75
  208.6 0.0 copy-done.1
  208.6 0.8 copy.76
  209.4 0.0 copy-done.10
  209.4 0.5 copy.77
  209.9 0.0 copy-done
  209.9 0.8 copy.78
  210.7 0.0 copy-done.9
  210.7 0.5 copy.79
  (5 shorter events, 0.0 us)
Async XLA Ops:
  197.4 1.9 copy-start.4
  199.4 0.8 copy-start.16
  199.4 1.9 copy-start.6
  200.2 0.6 copy-start.15
  201.3 1.0 copy-start.8
  201.3 1.7 copy-start.3
  202.9 0.8 copy-start.14
  202.9 1.3 copy-start.2
  204.3 0.8 copy-start.13
  204.3 2.7 %copy-start.5 = (f32[32,3072]{1,0:T(8,128)S(1)}, f32[32,3072]{1,0:T(8,128)}, u32[]{:S(2)}) copy-start(f32[32,3072]{1,0:T(8,128)} %get-tuple-element.84) | copy-start | bytes 1179652
  205.1 0.7 copy-start.12
  205.7 0.7 copy-start.11
  206.9 1.0 copy-start.7
  206.9 1.7 copy-start.1
  208.6 0.8 copy-start.10
  208.6 1.3 copy-start
  209.9 0.8 copy-start.9

commit v2 on v1

--- a/solution.py
+++ b/solution.py
@@ -337,16 +337,13 @@
 def block_kernel(rows, *refs):
     (
         x_ref, dy_ref, gain_ref, shift_ref, win_ref, wout_ref, wexp_ref, ebias_ref, wred_ref, rbias_ref,
-        mgain_ref, mshift_ref, min_ref, mout_ref, mexp_ref, mebias_ref, mred_ref, mrbias_ref,
-        rate_ref, decay_ref, cosr_ref, sinr_ref, cosb_ref, sinb_ref,
-        hout_ref, hgrad_ref,
-        ngain_ref, nshift_ref, nin_ref, nout_ref, nexp_ref, nebias_ref, nred_ref, nrbias_ref,
-        ugain_ref, ushift_ref, uin_ref, uout_ref, uexp_ref, uebias_ref, ured_ref, urbias_ref,
+        cosr_ref, sinr_ref, cosb_ref, sinb_ref,
+        hout_ref, hgrad_ref, ra_in, ra_exp, tred_ref, tout_ref, tile_ref,
         xg, dyg, xn, win, wexp, wred, wout, wz, pin, pexp,
-        q_s, k_s, vx, o_s, do_s, dkt, dvt, dfused, sbuf, mref, acc, dqacc,
+        q_s, k_s, vx, o_s, do_s, dkt, dvt, dfused, sbuf, lse, mref, acc, dqacc,
         act_s, de_s, pdn, sib_o, sib_d, r1_o, r2_o, r1_d, r2_d,
-        gin, gexp, gred, gout, gz, rz_in, rz_exp, rz_red, rz_out, ra_in, ra_exp,
-        vt, vecs, geb, sv, rv, zt, rzv,
+        gin, gexp, gred, gout, gz, rz_in, rz_exp, rz_red, rz_out, rb_in, rb_exp,
+        vt, vecs, geb, sums, sv, rv, zt, rzv,
         a2a_s, a2a_r, ag_s, ag_r, z_s, z_r, vz_s, vz_r, vp_s, vp_r, wo_s, wo_r,
         rs_s, rs_r, zr_s, zr_r, go_s, go_r, b_s, b_r, sp_s, sp_r, sz_s, sz_r,
     ) = refs
@@ -378,7 +375,12 @@
             device_id=(dd, ss), device_id_type=MESH,
         )
 
-    lanes = lax.broadcasted_iota(jnp.int32, (8, 128), 1)
+    barrier = pltpu.get_barrier_semaphore()
+    for m in range(1, NP):
+        pl.semaphore_signal(barrier, inc=1, device_id=(d, peer(m)), device_id_type=MESH)
+    for dz in range(1, NZ):
+        pl.semaphore_signal(barrier, inc=1, device_id=(lax.rem(d + dz, NZ), s), device_id_type=MESH)
+
     zrow = jnp.zeros((1, 96), F32)
     small = jnp.concatenate(
         [
@@ -392,33 +394,31 @@
     rows8 = lax.broadcasted_iota(jnp.int32, (8, 128), 0)
     ebias_row = jnp.broadcast_to(ebias_ref[...].astype(BF16).astype(F32), (8, 128))
     vt[s, d] = jnp.where(rows8 == 3, ebias_row, small)
-
+    wz[d] = wout_ref[...].astype(BF16)
+    xg[pl.ds(aligned(rows * s, rows), rows), :] = x_ref[...]
     own_rows = aligned(32 * (8 * d + s), 32)
-    for m in range(NP):
-        t = peer(m)
-        j = pair_of(t)
-        for part in range(3):
-            piece = win_ref[:, pl.ds(aligned(128 * j + 1024 * part, 128), 128)].astype(BF16)
-            if m == 0:
-                win[pl.ds(own_rows, 32), 128 * part : 128 * (part + 1)] = piece
-            else:
-                pin[m, :, 128 * part : 128 * (part + 1)] = piece
-        for e in range(NZ):
-            piece = wexp_ref[:, pl.ds(aligned(128 * (8 * e + t), 128), 128)].astype(BF16)
-            if m == 0:
-                wexp[pl.ds(own_rows, 32), 128 * e : 128 * (e + 1)] = piece
-            else:
-                pexp[m, :, 128 * e : 128 * (e + 1)] = piece
-    wz[d] = wout_ref[...].astype(BF16)
-    wred[pl.ds(aligned(128 * d, 128), 128), :] = wred_ref[...].astype(BF16)
-    xg[pl.ds(aligned(rows * s, rows), rows), :] = x_ref[...]
-    dyg[pl.ds(aligned(rows * s, rows), rows), :] = dy_ref[...]
-
-    barrier = pltpu.get_barrier_semaphore()
-    for m in range(1, NP):
-        pl.semaphore_signal(barrier, inc=1, device_id=(d, peer(m)), device_id_type=MESH)
-    for dz in range(1, NZ):
-        pl.semaphore_signal(barrier, inc=1, device_id=(lax.rem(d + dz, NZ), s), device_id_type=MESH)
+
+    def pack_in():
+        for m in range(NP):
+            j = pair_of(peer(m))
+            for part in range(3):
+                piece = win_ref[:, pl.ds(aligned(128 * j + 1024 * part, 128), 128)].astype(BF16)
+                if m == 0:
+                    win[pl.ds(own_rows, 32), 128 * part : 128 * (part + 1)] = piece
+                else:
+                    pin[m, :, 128 * part : 128 * (part + 1)] = piece
+
+    def pack_exp():
+        for m in range(NP):
+            t = peer(m)
+            for e in range(NZ):
+                piece = wexp_ref[:, pl.ds(aligned(128 * (8 * e + t), 128), 128)].astype(BF16)
+                if m == 0:
+                    wexp[pl.ds(own_rows, 32), 128 * e : 128 * (e + 1)] = piece
+                else:
+                    pexp[m, :, 128 * e : 128 * (e + 1)] = piece
+
+    pack_in()
     pl.semaphore_wait(barrier, NP - 1 + NZ - 1)
 
     def a2a_msg(which, m):
@@ -522,9 +522,11 @@
     z_send(3)
     for i in (1, 2, 0):
         ag_start(0, i)
+    pack_exp()
     for m in range(1, NP):
         a2a_msg(1, m).start()
-
+    wred[pl.ds(aligned(128 * d, 128), 128), :] = wred_ref[...].astype(BF16)
+    dyg[pl.ds(aligned(rows * s, rows), rows), :] = dy_ref[...]
     for i in range(1, NZ):
         vz_copy(i, True).wait_recv()
     for m in range(1, NP):
@@ -535,7 +537,12 @@
     for m in range(1, NP):
         a2a_arrived(1, m)
     z_send(1)
-    z_send(2)
+
+    def wo_copy(m, incoming):
+        src = wz.at[lax.rem(peer(m), 4)]
+        r = lax.rem(peer(m), 4) if incoming else quad
+        dst = wout.at[pl.ds(aligned(32 * r, 32), 32)]
+        return rc(src, dst, wo_s.at[m], wo_r.at[m], d, peer(m))
 
     for m in range(1, NP):
         vp_copy(m, True).wait_recv()
@@ -593,11 +600,12 @@
     ag_arrived(0, 0)
     norm_block(peer(1))
     norm_block(peer(2))
-    norm_block(peer(4))
     ag_arrived(0, 6)
     ag_start(0, 7)
     ag_arrived(0, 5)
     ag_start(0, 8)
+    norm_block(peer(4))
+    z_forward(3)
     ag_arrived(0, 3)
     norm_block(peer(3))
     ag_arrived(0, 4)
@@ -606,28 +614,18 @@
     ag_arrived(0, 7)
     ag_arrived(0, 8)
     norm_block(peer(7))
-
-    z_forward(3)
     z_arrived(3)
-
-    def wo_copy(m, incoming):
-        src = wz.at[lax.rem(peer(m), 4)]
-        r = lax.rem(peer(m), 4) if incoming else quad
-        dst = wout.at[pl.ds(aligned(32 * r, 32), 32)]
-        return rc(src, dst, wo_s.at[m], wo_r.at[m], d, peer(m))
-
     for m in range(1, 4):
         wo_copy(m, False).start()
     wout[pl.ds(aligned(32 * quad, 32), 32), :] = wz[quad]
-
+    z_forward(0)
+    z_send(2)
     ag_arrived(1, 1)
     ag_start(1, 5)
     ag_start(1, 3)
     ag_arrived(1, 2)
     ag_start(1, 6)
     ag_start(1, 4)
-
-    z_forward(0)
     z_arrived(0)
 
     def qkv_step(b, carry):
@@ -640,50 +638,34 @@
         return carry
 
     lax.fori_loop(0, NP, qkv_step, 0)
-    ag_arrived(1, 6)
-    ag_start(1, 7)
-    ag_arrived(1, 5)
-    ag_start(1, 8)
-    for i in (0, 3, 4, 7, 8):
-        ag_arrived(1, i)
-    for m in range(1, 4):
-        wo_copy(m, True).wait_recv()
-
-    def do_step(b, carry):
-        at = aligned(rows * b, rows)
-        do_s[pl.ds(at, rows), :] = dot_nt(dyg[pl.ds(at, rows), :], wout[...]).astype(BF16)
-        return carry
-
-    lax.fori_loop(0, NP, do_step, 0)
-
     KB = 2 * rows
 
-    def weights_at(h, j):
-        return pl.ds(aligned(rows * (NP // 2 * h + j), rows), rows)
-
-    dkt[...] = jnp.zeros_like(dkt)
-    dvt[...] = jnp.zeros_like(dvt)
+    def wide(tile):
+        return jnp.concatenate([tile] * (KB // 128), axis=1)
+
+    def fold(v):
+        out = v[:, :128]
+        for c in range(1, KB // 128):
+            out = jnp.maximum(out, v[:, 128 * c : 128 * (c + 1)])
+        return out
+
+    def by_head(block):
+        zero = jnp.zeros_like(block)
+        return jnp.where(low_head, block, zero), jnp.where(low_head, zero, block)
+
+    def hidden(i, j):
+        query = rows * i + lax.broadcasted_iota(jnp.int32, (rows, KB), 0)
+        key = KB * j + lax.broadcasted_iota(jnp.int32, (rows, KB), 1)
+        return key > query
 
     def attend_step(i, carry):
         at = aligned(rows * i, rows)
-        count = lax.div(i, 2) + 1
-        qi = q_s[pl.ds(at, rows), :]
-        zero = jnp.zeros_like(qi)
-        qh = (jnp.where(low_head, qi, zero), jnp.where(low_head, zero, qi))
-
-        def fold(v):
-            out = v[:, :128]
-            for c in range(1, KB // 128):
-                out = jnp.maximum(out, v[:, 128 * c : 128 * (c + 1)])
-            return out
-
-        last = count - 1
-        ka = aligned(KB * last, KB)
-        kj = k_s[pl.ds(ka, KB), :]
-        query = at + lax.broadcasted_iota(jnp.int32, (rows, KB), 0)
-        key = ka + lax.broadcasted_iota(jnp.int32, (rows, KB), 1)
+        last = lax.div(i, 2)
+        qh = by_head(q_s[pl.ds(at, rows), :])
+        kj = k_s[pl.ds(aligned(KB * last, KB), KB), :]
+        mask = hidden(i, last)
         for h in range(2):
-            sc = jnp.where(key <= query, dot_nt(qh[h], kj), masked_score)
+            sc = jnp.where(mask, masked_score, dot_nt(qh[h], kj))
             sbuf[h, last] = sc
             mref[h] = fold(sc)
 
@@ -696,76 +678,132 @@
             return c2
 
         lax.fori_loop(0, last, scores, 0)
-        top = [jnp.max(mref[h], axis=1, keepdims=True) for h in range(2)]
         for h in range(2):
-            mref[h] = jnp.broadcast_to(top[h], (rows, 128))
+            mref[h] = jnp.broadcast_to(jnp.max(mref[h], axis=1, keepdims=True), (rows, 128))
             acc[h] = jnp.zeros((rows, 256), F32)
 
         def weigh(j, c2):
             vj = vx[pl.ds(aligned(KB * j, KB), KB), :]
             for h in range(2):
-                pj = jnp.exp(sbuf[h, j] - mref[h][:, :1]).astype(BF16)
-                act_s[weights_at(h, j), :] = pj
+                pj = jnp.exp(sbuf[h, j] - wide(mref[h])).astype(BF16)
                 acc[h] = acc[h] + dot(pj, vj)
             return c2
 
-        lax.fori_loop(0, count, weigh, 0)
-        recip = [1.0 / acc[h][:, 128:] for h in range(2)]
-        scale = jnp.where(low_head, recip[0], recip[1])
-        of = jnp.where(low_head, acc[0][:, :128], acc[1][:, :128]) * scale
-        o_s[pl.ds(at, rows), :] = of.astype(BF16)
+        lax.fori_loop(0, last + 1, weigh, 0)
+        o_s[pl.ds(at, rows), :] = jnp.where(
+            low_head, acc[0][:, :128] / acc[0][:, 128:], acc[1][:, :128] / acc[1][:, 128:]
+        ).astype(BF16)
+        for h in range(2):
+            lse[h, pl.ds(at, rows), :] = mref[h] + jnp.log(acc[h][:, 128:])
+
+        @pl.when(i == 4)
+        def _():
+            z_forward(1)
+        return carry
+
+    lax.fori_loop(0, NP, attend_step, 0)
+    ag_arrived(1, 6)
+    ag_start(1, 7)
+    ag_arrived(1, 5)
+    ag_start(1, 8)
+    dkt[...] = jnp.zeros_like(dkt)
+    dvt[...] = jnp.zeros_like(dvt)
+
+    def attend_back(i):
+        at = aligned(rows * i, rows)
+        last = lax.div(i, 2)
+        qi = q_s[pl.ds(at, rows), :]
         doi = do_s[pl.ds(at, rows), :]
         dof = doi.astype(F32)
-        prod = dof * of
-        delta = (
-            jnp.sum(jnp.where(low_head, prod, 0.0), axis=1, keepdims=True),
-            jnp.sum(jnp.where(low_head, 0.0, prod), axis=1, keepdims=True),
-        )
+        qh = by_head(qi)
+        doh = by_head(doi)
+        qt = jnp.transpose(qi.astype(F32)).astype(BF16)
+        dot_t = jnp.transpose(dof).astype(BF16)
+        prod = dof * o_s[pl.ds(at, rows), :].astype(F32)
+        parts = by_head(prod)
         for h in range(2):
-            mref[h] = jnp.broadcast_to(delta[h], (rows, 128))
+            mref[h] = jnp.broadcast_to(jnp.sum(parts[h], axis=1, keepdims=True), (rows, 128))
             dqacc[h] = jnp.zeros((rows, 128), F32)
-        doh = (jnp.where(low_head, doi, zero), jnp.where(low_head, zero, doi))
-        dot_t = jnp.transpose(dof * scale).astype(BF16)
-        qt = jnp.transpose(qi.astype(F32) * scale).astype(BF16)
-
-        def back(j, c2):
+
+        def unit(j, mask):
             ja = aligned(KB * j, KB)
             kk = k_s[pl.ds(ja, KB), :]
             vj = vx[pl.ds(ja, KB), :128]
             for h in range(2):
                 hs = slice(HD * h, HD * (h + 1))
-                pj = act_s[weights_at(h, j), :]
-                dp = dot_nt(doh[h], vj)
-                ds = (pj.astype(F32) * (dp - mref[h][:, :1])).astype(BF16)
+                p = jnp.exp(dot_nt(qh[h], kk) - wide(lse[h, pl.ds(at, rows), :]))
+                if mask is not None:
+                    p = jnp.where(mask, 0.0, p)
+                ds = (p * (dot_nt(doh[h], vj) - wide(mref[h]))).astype(BF16)
                 dqacc[h] = dqacc[h] + dot(ds, kk)
                 dkt[hs, pl.ds(ja, KB)] = dkt[hs, pl.ds(ja, KB)] + dot(qt[hs, :], ds)
-                dvt[hs, pl.ds(ja, KB)] = dvt[hs, pl.ds(ja, KB)] + dot(dot_t[hs, :], pj)
+                dvt[hs, pl.ds(ja, KB)] = dvt[hs, pl.ds(ja, KB)] + dot(dot_t[hs, :], p.astype(BF16))
+
+        def free(j, c2):
+            unit(j, None)
             return c2
 
-        lax.fori_loop(0, count, back, 0)
-        dq = jnp.where(low_head, dqacc[0], dqacc[1]) * (scale * HD**-0.5)
+        lax.fori_loop(0, last, free, 0)
+        unit(last, hidden(i, last))
+        dq = jnp.where(low_head, dqacc[0], dqacc[1]) * HD**-0.5
         dfused[pl.ds(at, rows), :128] = turn(dq, i, -1.0).astype(BF16)
 
-        @pl.when(i == 3)
-        def _():
-            z_forward(1)
-
-        @pl.when(i == 6)
+    for i in (0, 3, 4, 7, 8):
+        ag_arrived(1, i)
+    for m in range(1, 4):
+        wo_copy(m, True).wait_recv()
+
+    def loop(n, f):
+        def step(i, carry):
+            f(i)
+            return carry
+        lax.fori_loop(0, n, step, 0)
+
+    def do_block(b):
+        at = aligned(rows * b, rows)
+        do_s[pl.ds(at, rows), :] = dot_nt(dyg[pl.ds(at, rows), :], wout[...]).astype(BF16)
+
+    loop(NP, do_block)
+    gout[...] = dot_tn(o_s[...], dyg[...]).astype(BF16)
+
+    def go_copy(m, incoming):
+        t4 = lax.rem(peer(m), 4)
+        src = gout.at[pl.ds(aligned(32 * t4, 32), 32)]
+        dst = gz.at[t4 if incoming else quad]
+        return rc(src, dst, go_s.at[m], go_r.at[m], d, peer(m))
+
+    for m in range(1, 4):
+        go_copy(m, False).start()
+    gz[quad] = gout[pl.ds(aligned(32 * quad, 32), 32), :]
+    early = 2
+
+    def back_early(step):
+        attend_back(NP - 1 - step)
+
+        @pl.when(step == 0)
         def _():
             z_forward(2)
-        return carry
-
-    lax.fori_loop(0, NP, attend_step, 0)
-
-    def kv_step(b, carry):
+
+    loop(early, back_early)
+    z_arrived(1)
+    z_arrived(2)
+
+    eb = jnp.concatenate([vt[s, dd, 3:4, :] for dd in range(NZ)], axis=1)
+    geb[...] = jnp.zeros_like(geb)
+    sums[...] = jnp.zeros_like(sums)
+    sums[2:3, :] = jnp.sum(dy_ref[...].astype(F32), axis=0, keepdims=True)
+
+    def ffn_block(b):
         at = aligned(rows * b, rows)
-        dk = jnp.transpose(dkt[:, pl.ds(at, rows)])
-        dv = jnp.transpose(dvt[:, pl.ds(at, rows)])
-        dfused[pl.ds(at, rows), 128:256] = turn(dk, b, -1.0).astype(BF16)
-        dfused[pl.ds(at, rows), 256:] = dv.astype(BF16)
-        return carry
-
-    lax.fori_loop(0, NP, kv_step, 0)
+        e = dot(xn[pl.ds(at, rows), :], wexp[...]) + eb
+        up = dot_nt(dyg[pl.ds(at, rows), :], wred[...])
+        a, slope = gelu_pair(e)
+        act_s[pl.ds(at, rows), :] = a.astype(BF16)
+        de = (up * slope).astype(BF16)
+        de_s[pl.ds(at, rows), :] = de
+        geb[...] = geb[...] + jnp.sum(de.astype(F32).reshape(rows // 8, 8, 4 * 128), axis=0)
+
+    loop(NP, ffn_block)
 
     GVIEW = (
         lambda b: gin.at[pl.ds(aligned(256 * b, 256), 256)],
@@ -845,10 +883,6 @@
             def _():
                 zr_copy(a, dest, dest, d, dest).wait_send()
 
-    def gin_block(b):
-        at = aligned(256 * b, 256)
-        gin[pl.ds(at, 256), :] = dot_tn(xn[:, pl.ds(at, 256)], dfused[...]).astype(BF16)
-
     def gexp_block(b):
         at = aligned(256 * b, 256)
         gexp[pl.ds(at, 256), :] = dot_tn(xn[:, pl.ds(at, 256)], de_s[...]).astype(BF16)
@@ -857,56 +891,24 @@
         at = aligned(128 * b, 128)
         gred[pl.ds(at, 128), :] = dot_tn(act_s[:, pl.ds(at, 128)], dyg[...]).astype(BF16)
 
-    def loop(n, f):
-        def step(i, carry):
-            f(i)
-            return carry
-        lax.fori_loop(0, n, step, 0)
-
-    loop(NZ, gin_block)
-    zr_first(0)
-    zr_send(0)
-    gout[...] = dot_tn(o_s[...], dyg[...]).astype(BF16)
-
-    def go_copy(m, incoming):
-        t4 = lax.rem(peer(m), 4)
-        src = gout.at[pl.ds(aligned(32 * t4, 32), 32)]
-        dst = gz.at[t4 if incoming else quad]
-        return rc(src, dst, go_s.at[m], go_r.at[m], d, peer(m))
-
-    for m in range(1, 4):
-        go_copy(m, False).start()
-    gz[quad] = gout[pl.ds(aligned(32 * quad, 32), 32), :]
-
-    z_arrived(1)
-    z_arrived(2)
-    eb = jnp.concatenate([vt[s, dd, 3:4, :] for dd in range(NZ)], axis=1)
-    geb[...] = jnp.zeros_like(geb)
-
-    def ffn_block(b):
-        at = aligned(rows * b, rows)
-        e = dot(xn[pl.ds(at, rows), :], wexp[...]) + eb
-        up = dot_nt(dyg[pl.ds(at, rows), :], wred[...])
-        a, slope = gelu_pair(e)
-        act_s[pl.ds(at, rows), :] = a.astype(BF16)
-        de = (up * slope).astype(BF16)
-        de_s[pl.ds(at, rows), :] = de
-        geb[...] = geb[...] + jnp.sum(de.astype(F32).reshape(rows // 8, 8, 4 * 128), axis=0)
-
-    loop(NP, ffn_block)
+    def dest_send(a, dest):
+        for src, via, to in COMB:
+            if to == dest:
+                @pl.when(d == src)
+                def _():
+                    zr_copy(a, to, via, via, to).start()
+
+        @pl.when(zr_direct(dest))
+        def _():
+            zr_copy(a, dest, dest, d, dest).start()
+
+    for dest in (3, 0, 2, 1):
+        gred_block(dest)
+        dest_send(2, dest)
     for m in range(1, 4):
         go_copy(m, True).wait_recv()
-    zr_first(3)
-    zr_send(3)
-    zr_join(0)
-    loop(NZ, gred_block)
-    zr_first(2)
-    zr_send(2)
-    zr_join(3)
-    loop(NZ, gexp_block)
-    zr_first(1)
-    zr_send(1)
-    zr_join(2)
+    for dest in (3, 0, 2, 1):
+        dest_send(3, dest)
 
     for i in range(9):
         ag_copy(0, i, False).wait_send()
@@ -919,9 +921,10 @@
 
     def dn_block(b):
         at = aligned(rows * b, rows)
-        pdn[pl.ds(at, rows), :] = (
-            dot_nt(de_s[pl.ds(at, rows), :], wexp[...]) + dot_nt(dfused[pl.ds(at, rows), :], win[...])
-        ).astype(BF16)
+        dn = dot_nt(de_s[pl.ds(at, rows), :], wexp[...]) + dot_nt(dfused[pl.ds(at, rows), :], win[...])
+        pdn[pl.ds(at, rows), :] = dn.astype(BF16)
+        sums[0:1, :] = sums[0:1, :] + jnp.sum(dn * xn[pl.ds(at, rows), :].astype(F32), axis=0, keepdims=True)
+        sums[1:2, :] = sums[1:2, :] + jnp.sum(dn, axis=0, keepdims=True)
 
     RS = ((pout, sib_o, r1_o, r2_o), (pdn, sib_d, r1_d, r2_d))
 
@@ -949,71 +952,102 @@
             ref[...] = (ref[...].astype(F32) + came[pl.ds(aligned(64 * c, 64), 64), :].astype(F32)).astype(BF16)
         loop(n // 64, step)
 
-    def rs_one(w):
+    def rs_across(w):
         rs_copy(w, 0).wait_recv()
         add_into(w, 6, 0, rows, RS[w][1].at[0])
         rs_copy(w, 4).start()
         rs_copy(w, 5).start()
-        rs_copy(w, 1).wait_recv()
-        add_into(w, 2, 0, rows, RS[w][1].at[1])
-        rs_copy(w, 2).wait_recv()
-        add_into(w, 4, 0, rows, RS[w][1].at[2])
-
-    def rs_two(w):
-        rs_copy(w, 5).wait_recv()
-        add_into(w, 2, half, half, RS[w][2].at[1])
-        rs_copy(w, 6).start()
-        rs_copy(w, 4).wait_recv()
-        add_into(w, 4, 0, half, RS[w][2].at[0])
-        rs_copy(w, 7).start()
-        rs_copy(w, 3).wait_recv()
-
-    def rs_three(w):
-        rs_copy(w, 6).wait_recv()
-        rs_copy(w, 7).wait_recv()
-
-    def rs_total(w, c):
-        at = aligned(64 * c, 64)
-        own = RS[w][0][pl.ds(aligned(rows * s + 64 * c, 64), 64), :].astype(F32)
-        own = own + RS[w][1][3, pl.ds(at, 64), :].astype(F32)
-        own = own + RS[w][3][0, pl.ds(at, 64), :].astype(F32)
-        return own + RS[w][3][1, pl.ds(at, 64), :].astype(F32)
+
+    def rs_pair(w, which):
+        rs_copy(w, 1 + which).wait_recv()
+        add_into(w, (2, 4)[which], 0, rows, RS[w][1].at[1 + which])
+
+    def rs_near(w, which):
+        rs_copy(w, 5 - which).wait_recv()
+        add_into(w, (2, 4)[which], (half, 0)[which], half, RS[w][2].at[1 - which])
+        rs_copy(w, 6 + which).start()
+
+    def rs_last(w):
+        for i in (3, 6, 7):
+            rs_copy(w, i).wait_recv()
 
     for i, m in enumerate((7, 3, 5, 1)):
         out_block(peer(m))
         rs_copy(0, i).start()
+    for dest in (3, 0, 2, 1):
+        gexp_block(dest)
+        dest_send(1, dest)
     for m in (6, 2, 4, 0):
         out_block(peer(m))
-    zr_join(1)
-    rs_one(0)
-    for i, m in enumerate((7, 3, 5, 1)):
+
+    def back_late(step):
+        attend_back(NP - 1 - early - step)
+
+        @pl.when(step == 0)
+        def _():
+            rs_across(0)
+            zr_join(2)
+
+        @pl.when(step == 1)
+        def _():
+            rs_pair(0, 0)
+            rs_pair(0, 1)
+            zr_join(3)
+
+        @pl.when(step == 2)
+        def _():
+            rs_near(0, 0)
+            rs_near(0, 1)
+            zr_join(1)
+
+    loop(NP - early, back_late)
+
+    def kv_block(b):
+        at = aligned(rows * b, rows)
+        dk = jnp.transpose(dkt[:, pl.ds(at, rows)])
+        dv = jnp.transpose(dvt[:, pl.ds(at, rows)])
+        dfused[pl.ds(at, rows), 128:256] = turn(dk, b, -1.0).astype(BF16)
+        dfused[pl.ds(at, rows), 256:] = dv.astype(BF16)
+
+    loop(NP, kv_block)
+
+    def gin_block(b):
+        at = aligned(256 * b, 256)
+        gin[pl.ds(at, 256), :] = dot_tn(xn[:, pl.ds(at, 256)], dfused[...]).astype(BF16)
+
+    for dest in (3, 0):
+        gin_block(dest)
+        dest_send(0, dest)
+    dn_block(peer(7))
+    rs_copy(1, 0).start()
+    for dest in (2, 1):
+        gin_block(dest)
+        dest_send(0, dest)
+    for i, m in ((1, 3), (2, 5), (3, 1)):
         dn_block(peer(m))
         rs_copy(1, i).start()
-    rs_two(0)
-    for m in (6, 2, 4, 0):
-        dn_block(peer(m))
-    rs_one(1)
-    rs_three(0)
-
-    def out_final(c):
-        at = aligned(64 * c, 64)
-        hout_ref[pl.ds(at, 64), :] = (
-            x_ref[pl.ds(at, 64), :].astype(F32) + rs_total(0, c) + vecs[2:3, :]
-        ).astype(BF16)
-
-    loop(rows // 64, out_final)
-    rs_two(1)
-
-    keep = 1.0 - decay_ref[0]
-    rate = rate_ref[0]
-    inv_count = 0.5 / NZ
-
-    def update(w_ref, m_ref, n_ref, u_ref, index, grad):
-        mom = 0.5 * m_ref[index] + grad * inv_count
-        n_ref[index] = mom
-        u_ref[index] = keep * w_ref[index] - rate * mom
-
-    def total_rows(a, n, width):
+    zr_join(0)
+    dn_block(peer(6))
+    rs_across(1)
+    dn_block(peer(2))
+    rs_pair(1, 0)
+    dn_block(peer(4))
+    rs_pair(1, 1)
+    dn_block(s)
+    for yy in range(2):
+        for dd in range(NZ):
+            group = 2 * dd + yy
+            sv[yy, dd] = sums[:, 128 * group : 128 * (group + 1)]
+
+    def sp_copy(m):
+        return rc(sv.at[lax.div(peer(m), 4)], rv.at[m], sp_s.at[m], sp_r.at[m], d, peer(m))
+
+    for m in range(1, NP):
+        sp_copy(m).start()
+
+    geb_row = jnp.sum(geb[...], axis=0, keepdims=True)
+
+    def total_rows(a, n):
         ref, use = zr_total(a)
 
         def step(c):
@@ -1024,21 +1058,38 @@
 
     def back_copy(which, m, incoming):
         src = (gin, gexp)[which].at[pl.ds(aligned(256 * d + 32 * peer(m), 32), 32)]
-        dst = (ra_in, ra_exp)[which].at[m]
+        dst = (rb_in, rb_exp)[which].at[m]
         return rc(src, dst, b_s.at[which, m], b_r.at[which, m], d, peer(m))
 
-    total_rows(0, 256, 384)
-    for m in range(1, NP):
-        back_copy(0, m, False).start()
-
-    ref_o, use_o = zr_total(3)
-    update(wout_ref, mout_ref, nout_ref, uout_ref, ..., zr_sum(3, use_o, ref_o[...].astype(F32), 0, 32))
-
-    rs_three(1)
-    sv0 = jnp.zeros((8, 1024), F32)
-    geb_row = jnp.sum(geb[...], axis=0, keepdims=True)
-
-    def grad_final(c, carry):
+    total_rows(1, 256)
+    for m in range(1, NP):
+        back_copy(1, m, False).start()
+    rs_near(1, 0)
+    rs_near(1, 1)
+
+    ref_r, use_r = zr_total(2)
+
+    def red_total(c):
+        at = aligned(32 * c, 32)
+        tred_ref[pl.ds(at, 32), :] = zr_sum(2, use_r, ref_r[pl.ds(at, 32), :].astype(F32), at, 32)
+    loop(4, red_total)
+    rs_last(0)
+
+    def out_final(c):
+        at = aligned(32 * c, 32)
+        hout_ref[pl.ds(at, 32), :] = (
+            x_ref[pl.ds(at, 32), :].astype(F32) + rs_total32(0, c) + vecs[2:3, :]
+        ).astype(BF16)
+
+    def rs_total32(w, c):
+        at = aligned(32 * c, 32)
+        own = RS[w][0][pl.ds(aligned(rows * s + 32 * c, 32), 32), :].astype(F32)
+        own = own + RS[w][1][3, pl.ds(at, 32), :].astype(F32)
+        own = own + RS[w][3][0, pl.ds(at, 32), :].astype(F32)
+        return own + RS[w][3][1, pl.ds(at, 32), :].astype(F32)
+
+    loop(rows // 32, out_final)
+    def grad_final(c):
         at = aligned(32 * c, 32)
         dn = rs_total32(1, c)
         unit, inv = unit_of(x_ref[pl.ds(at, 32), :])
@@ -1049,43 +1100,6 @@
         ) + dyf
         hgrad_ref[pl.ds(at, 32), :] = hg.astype(BF16)
 
-        def fold8(v):
-            out = v[0:8]
-            for r in range(8, 32, 8):
-                out = out + v[r : r + 8]
-            return out
-        return (carry[0] + fold8(dn * unit), carry[1] + fold8(dn), carry[2] + fold8(dyf))
-
-    def rs_total32(w, c):
-        at = aligned(32 * c, 32)
-        own = RS[w][0][pl.ds(aligned(rows * s + 32 * c, 32), 32), :].astype(F32)
-        own = own + RS[w][1][3, pl.ds(at, 32), :].astype(F32)
-        own = own + RS[w][3][0, pl.ds(at, 32), :].astype(F32)
-        return own + RS[w][3][1, pl.ds(at, 32), :].astype(F32)
-
-    sums = lax.fori_loop(0, rows // 32, grad_final, (sv0, sv0, sv0))
-    row_sums = [jnp.sum(v, axis=0, keepdims=True) for v in sums]
-    stacked = jnp.concatenate(row_sums + [jnp.zeros((5, 1024), F32)], axis=0)
-    for yy in range(2):
-        for dd in range(NZ):
-            group = 2 * dd + yy
-            sv[yy, dd] = stacked[:, 128 * group : 128 * (group + 1)]
-
-    def sp_copy(m):
-        return rc(sv.at[lax.div(peer(m), 4)], rv.at[m], sp_s.at[m], sp_r.at[m], d, peer(m))
-
-    for m in range(1, NP):
-        sp_copy(m).start()
-
-    ref_r, use_r = zr_total(2)
-
-    def red_update(c):
-        at = aligned(16 * c, 16)
-        update(
-            wred_ref, mred_ref, nred_ref, ured_ref, (pl.ds(at, 16), slice(None)),
-            zr_sum(2, use_r, ref_r[pl.ds(at, 16), :].astype(F32), at, 16),
-        )
-    loop(8, red_update)
     for m in range(1, NP):
         sp_copy(m).wait_recv()
     tiles = sv[ybit]
@@ -1100,49 +1114,29 @@
 
     for i in range(1, NZ):
         sz_copy(i, False).start()
-
-    total_rows(1, 256, 512)
-    for m in range(1, NP):
-        back_copy(1, m, False).start()
-
-    def strip_in(m, grads):
-        j = pair_of(peer(m))
-        for prt in range(3):
-            cols = pl.ds(aligned(128 * j + 1024 * prt, 128), 128)
-            update(win_ref, min_ref, nin_ref, uin_ref, (slice(None), cols), grads[:, 128 * prt : 128 * (prt + 1)])
-
-    def strip_exp(m, grads):
-        t = peer(m)
-        for e in range(NZ):
-            cols = pl.ds(aligned(128 * (8 * e + t), 128), 128)
-            update(wexp_ref, mexp_ref, nexp_ref, uexp_ref, (slice(None), cols), grads[:, 128 * e : 128 * (e + 1)])
+    total_rows(0, 256)
+    for m in range(1, NP):
+        back_copy(0, m, False).start()
+    rs_last(1)
+    loop(rows // 32, grad_final)
+    ref_o, use_o = zr_total(3)
+    tout_ref[...] = zr_sum(3, use_o, ref_o[...].astype(F32), 0, 32)
 
     mine = pl.ds(aligned(256 * d + 32 * s, 32), 32)
-    strip_in(0, gin[mine, :].astype(F32))
+    ra_exp[0] = gexp[mine, :]
+    ra_in[0] = gin[mine, :]
+    for m in range(1, NP):
+        back_copy(1, m, True).wait_recv()
+        ra_exp[m] = rb_exp[m]
     for m in range(1, NP):
         back_copy(0, m, True).wait_recv()
-        strip_in(m, ra_in[m].astype(F32))
-
+        ra_in[m] = rb_in[m]
     for i in range(1, NZ):
         sz_copy(i, True).wait_recv()
     tile = zt[d]
     for i in range(1, NZ):
         tile = tile + rzv[i]
-    update(ebias_ref, mebias_ref, nebias_ref, uebias_ref, ..., tile[3:4, :])
-    tile = pltpu.roll(tile, lax.rem(128 - 32 * quad, 128), 1)
-    for r, (w, mo, n, u) in enumerate(
-        (
-            (gain_ref, mgain_ref, ngain_ref, ugain_ref),
-            (shift_ref, mshift_ref, nshift_ref, ushift_ref),
-            (rbias_ref, mrbias_ref, nrbias_ref, urbias_ref),
-        )
-    ):
-        update(w, mo, n, u, ..., tile[r : r + 1, :32])
-
-    strip_exp(0, gexp[mine, :].astype(F32))
-    for m in range(1, NP):
-        back_copy(1, m, True).wait_recv()
-        strip_exp(m, ra_exp[m].astype(F32))
+    tile_ref[...] = jnp.where(rows8 == 3, tile, pltpu.roll(tile, lax.rem(128 - 32 * quad, 128), 1))
 
     for m in range(1, NP):
         a2a_msg(0, m).wait_send()
@@ -1167,6 +1161,51 @@
         zr_sent(a)
 
 
+def update_kernel(*refs):
+    weights, moments = refs[0:8], refs[8:16]
+    rate_ref, decay_ref, hout_in, hgrad_in, gin, gexp, gred, gout, tile = refs[16:25]
+    hout, hgrad = refs[25:27]
+    new_moments, new_weights = refs[27:35], refs[35:43]
+    s = lax.axis_index("seq")
+    keep = 1.0 - decay_ref[0]
+    rate = rate_ref[0]
+
+    def update(k, index, grad):
+        moment = 0.5 * moments[k][index] + grad * (0.5 / NZ)
+        new_moments[k][index] = moment
+        new_weights[k][index] = keep * weights[k][index] - rate * moment
+
+    hout[...] = hout_in[...]
+    hgrad[...] = hgrad_in[...]
+    gain = weights[0][...].astype(BF16).astype(F32)
+    shift = weights[1][...].astype(BF16).astype(F32)
+    shift_grad = tile[1:2, :32]
+    update(0, ..., (tile[0:1, :32] - shift * shift_grad) / gain)
+    update(1, ..., shift_grad)
+    update(7, ..., tile[2:3, :32])
+    update(5, ..., tile[3:4, :])
+    update(6, ..., gred[...])
+    update(3, ..., gout[...])
+    core = lax.rem(s, 2)
+    xbit = lax.rem(lax.div(s, 2), 2)
+    ybit = lax.div(s, 4)
+    for m in range(NP):
+        t = s
+        if m & 1:
+            t = t + (1 - 2 * core)
+        if m & 2:
+            t = t + 2 * (1 - 2 * xbit)
+        if m & 4:
+            t = t + 4 * (1 - 2 * ybit)
+        pair = 2 * lax.rem(t, 4) + lax.div(t, 4)
+        for part in range(3):
+            cols = pl.ds(aligned(128 * pair + 1024 * part, 128), 128)
+            update(2, (slice(None), cols), gin[m, :, 128 * part : 128 * (part + 1)].astype(F32))
+        for e in range(NZ):
+            cols = pl.ds(aligned(128 * (8 * e + t), 128), 128)
+            update(4, (slice(None), cols), gexp[m, :, 128 * e : 128 * (e + 1)].astype(F32))
+
+
 def fused_shards(*args):
     (hidden_in, out_cotangent), weights, moments = args[:2], args[2:10], args[10:18]
     rows = hidden_in.shape[1]
@@ -1182,6 +1221,7 @@
 
     shards_in = [flat(w) for w in weights]
     ff = weights[6].shape[0] * NZ
+    moments_in = [flat(m) for m in moments]
     shard_shapes = [jax.ShapeDtypeStruct(w.shape, F32) for w in shards_in]
     vm = pltpu.VMEM
     dma = pltpu.SemaphoreType.DMA
@@ -1191,7 +1231,7 @@
         vm((NP, 32, 384), BF16), vm((NP, 32, ff), BF16),
         vm((seq, 128), BF16), vm((seq, 128), BF16), vm((seq, 256), BF16), vm((seq, 128), BF16), vm((seq, 128), BF16),
         vm((128, seq), F32), vm((128, seq), F32), vm((seq, 384), BF16),
-        vm((2, NP // 2, rows, 2 * rows), F32),
+        vm((2, NP // 2, rows, 2 * rows), F32), vm((2, seq, 128), F32),
         vm((2, rows, 128), F32), vm((2, rows, 256), F32), vm((2, rows, 128), F32),
         vm((seq, ff), BF16), vm((seq, ff), BF16), vm((seq, D), BF16),
         vm((4, rows, D), BF16), vm((4, rows, D), BF16),
@@ -1199,7 +1239,7 @@
         vm((D, 384), BF16), vm((D, ff), BF16), vm((ff, D), BF16), vm((128, D), BF16), vm((NZ, 32, D), BF16),
         vm((NZ, 256, 384), BF16), vm((NZ, 256, ff), BF16), vm((NZ, 128, D), BF16), vm((NZ, 32, D), BF16),
         vm((NP, 32, 384), BF16), vm((NP, 32, ff), BF16),
-        vm((NP, NZ, 8, 128), F32), vm((8, D), F32), vm((8, ff), F32),
+        vm((NP, NZ, 8, 128), F32), vm((8, D), F32), vm((8, ff), F32), vm((8, D), F32),
         vm((2, NZ, 8, 128), F32), vm((NP, NZ, 8, 128), F32), vm((NZ, 8, 128), F32), vm((NZ, 8, 128), F32),
         dma((2, NP)), dma((2, NP)), dma((2, 9)), dma((2, 9)), dma((4, 5)), dma((4, 4)),
         dma((NZ,)), dma((NZ,)), dma((NP,)), dma((NP,)), dma((4,)), dma((4,)),
@@ -1213,20 +1253,32 @@
         block_kernel(rows, *refs)
 
     rows_shape = jax.ShapeDtypeStruct((rows, D), BF16)
-    outs = pl.pallas_call(
+    grads = pl.pallas_call(
         body,
-        out_shape=[rows_shape, rows_shape] + shard_shapes + shard_shapes,
-        in_specs=[in_vmem] * 18 + [in_smem] * 2 + [in_vmem] * 4,
-        out_specs=[in_vmem] * 18,
+        out_shape=[
+            rows_shape, rows_shape,
+            jax.ShapeDtypeStruct((NP, 32, 384), BF16), jax.ShapeDtypeStruct((NP, 32, ff), BF16),
+            jax.ShapeDtypeStruct((128, D), F32), jax.ShapeDtypeStruct((32, D), F32),
+            jax.ShapeDtypeStruct((8, 128), F32),
+        ],
+        in_specs=[in_vmem] * 14,
+        out_specs=[in_vmem] * 7,
         scratch_shapes=scratch,
         compiler_params=pltpu.CompilerParams(
             collective_id=0, has_side_effects=True, vmem_limit_bytes=63 * 2**20
         ),
         name="block_step",
     )(
-        hidden_in.reshape(rows, D), out_cotangent.reshape(rows, D), *shards_in,
-        *[flat(m) for m in moments], args[18], args[19], tables[0], tables[1], tables[2], tables[3],
-    )
+        hidden_in.reshape(rows, D), out_cotangent.reshape(rows, D), *shards_in, *tables,
+    )
+    outs = pl.pallas_call(
+        update_kernel,
+        out_shape=[rows_shape, rows_shape] + shard_shapes + shard_shapes,
+        in_specs=[in_vmem] * 16 + [in_smem] * 2 + [in_vmem] * 7,
+        out_specs=[in_vmem] * 18,
+        compiler_params=pltpu.CompilerParams(vmem_limit_bytes=63 * 2**20),
+        name="block_update",
+    )(*shards_in, *moments_in, args[18], args[19], *grads)
     small = [w.shape for w in weights]
     return (
         outs[0].reshape(hidden_in.shape),

time: 213 us -> 169 us (0.79)
  Pallas kernels: 195 us -> 167 us
  local copies, waits for them, and re-layouts: 13.8 us -> 0 us
    pallas_call x1 -> x2, Pallas kernels: 195 us -> 167 us  [the longest x1 161 us: fused_shards(): pl.pallas_call(body, out_shape=[rows_shape, rows_shape, jax.ShapeDtypeStr...]
    unnamed x52 -> x0, local copies, waits for them, and re-layouts: 13.8 us -> none
where the time goes in v2:
time: 169 us
  Pallas kernels  167 us (99%)
  between operations  2.13 us (1%)
    pallas_call x1, Pallas kernels, fused_shards(): pl.pallas_call(body, out_shape=[rows_shape, rows_shape, jax.ShapeDtypeStr...  161 us
    pallas_call x1, Pallas kernels, fused_shards(): pl.pallas_call(update_kernel, out_shape=[rows_shape, rows_shape] + shard_...  5.19 us

profile of v2, /device:TPU:13, one launch (start us, length us, event | category | flops | bytes accessed | tf_op | source)
XLA Modules:
  0.0 168.7 jit_solution(7458094298295321894)
XLA Ops:
  1.9 161.3 %block_step.1 = (bf16[256,1024]{1,0:T(8,128)(2,1)}, bf16[256,1024]{1,0:T(8,128)(2,1)}, bf16[8,32,384]{2,1,0:T(8,128)(2,1)}, bf16[8,32,512]{2,1,0:T(8,128)(2,1)},...) custom-call(bf16[256,1024]{1,0:T(8,128)(2,1)} %bitcast.20, bf16[256,1024]{1,0:T(8,128)(2,1)} %bitcast.21, ...), custom_call_target="tpu_custom_call" | custom-call | tf_op jit(solution)/shard_map/block_step/pallas_call | solution.py:1256
  163.3 5.2 %block_update.1 = (bf16[256,1024]{1,0:T(8,128)(2,1)}, bf16[256,1024]{1,0:T(8,128)(2,1)}, f32[1,32]{1,0:T(1,128)}, f32[1,32]{1,0:T(1,128)}, f32[32,3072]{1,0:T(8,...) custom-call(f32[1,32]{1,0:T(1,128)} %bitcast.23, ...), custom_call_target="tpu_custom_call" | custom-call | tf_op jit(solution)/shard_map/block_update/pallas_call | solution.py:1274

commit v3 on v2

--- a/solution.py
+++ b/solution.py
@@ -340,12 +340,12 @@
         cosr_ref, sinr_ref, cosb_ref, sinb_ref,
         hout_ref, hgrad_ref, ra_in, ra_exp, tred_ref, tout_ref, tile_ref,
         xg, dyg, xn, win, wexp, wred, wout, wz, pin, pexp,
-        q_s, k_s, vx, o_s, do_s, dkt, dvt, dfused, sbuf, lse, mref, acc, dqacc,
+        o_s, do_s, dkt, dvt, dfused, sbuf, lse, mref, acc,
         act_s, de_s, pdn, sib_o, sib_d, r1_o, r2_o, r1_d, r2_d,
         gin, gexp, gred, gout, gz, rz_in, rz_exp, rz_red, rz_out, rb_in, rb_exp,
-        vt, vecs, geb, sums, sv, rv, zt, rzv,
+        vt, vecs, ebs, geb, sums, sv, rv, zt, rzv,
         a2a_s, a2a_r, ag_s, ag_r, z_s, z_r, vz_s, vz_r, vp_s, vp_r, wo_s, wo_r,
-        rs_s, rs_r, zr_s, zr_r, go_s, go_r, b_s, b_r, sp_s, sp_r, sz_s, sz_r,
+        rs_s, rs_r, zr_s, zr_r, go_s, go_r, b_s, b_r, sp_s, sp_r, sz_s, sz_r, dy_sem,
     ) = refs
     pout = xg
     d = lax.axis_index("dp")
@@ -395,6 +395,8 @@
     ebias_row = jnp.broadcast_to(ebias_ref[...].astype(BF16).astype(F32), (8, 128))
     vt[s, d] = jnp.where(rows8 == 3, ebias_row, small)
     wz[d] = wout_ref[...].astype(BF16)
+    own_dy = pltpu.make_async_copy(dy_ref, dyg.at[pl.ds(aligned(rows * s, rows), rows)], dy_sem)
+    own_dy.start()
     xg[pl.ds(aligned(rows * s, rows), rows), :] = x_ref[...]
     own_rows = aligned(32 * (8 * d + s), 32)
 
@@ -483,11 +485,22 @@
                 z_wait_block(a, blk)
                 rc(ZVIEW[a](blk), ZVIEW[a](blk), z_s.at[a, 4], z_r.at[a, blk], dest, s).start()
 
-    def z_arrived(a):
+    PACE = ((0, 1), (3, 2))
+
+    def z_pace(a):
+        for at, blk in PACE:
+            @pl.when(d == at)
+            def _():
+                z_wait_block(a, blk)
+
+    def z_arrived(a, paced=False):
         for b in range(NZ):
             need = d != b
             for at, blk, dest in FWD:
                 if blk == b:
+                    need = need & (d != at)
+            for at, blk in PACE:
+                if paced and blk == b:
                     need = need & (d != at)
 
             @pl.when(need)
@@ -523,10 +536,7 @@
     for i in (1, 2, 0):
         ag_start(0, i)
     pack_exp()
-    for m in range(1, NP):
-        a2a_msg(1, m).start()
     wred[pl.ds(aligned(128 * d, 128), 128), :] = wred_ref[...].astype(BF16)
-    dyg[pl.ds(aligned(rows * s, rows), rows), :] = dy_ref[...]
     for i in range(1, NZ):
         vz_copy(i, True).wait_recv()
     for m in range(1, NP):
@@ -534,6 +544,18 @@
     for m in range(1, NP):
         a2a_arrived(0, m)
     z_send(0)
+    for m in range(1, NP):
+        a2a_msg(1, m).start()
+    z_forward(3)
+    z_pace(0)
+    z_forward(0)
+    z_send(2)
+    ag_arrived(0, 1)
+    ag_start(0, 5)
+    ag_start(0, 3)
+    ag_arrived(0, 2)
+    ag_start(0, 6)
+    ag_start(0, 4)
     for m in range(1, NP):
         a2a_arrived(1, m)
     z_send(1)
@@ -576,40 +598,34 @@
     first_rot = in_head < ROT // 2
     second_rot = (in_head >= ROT // 2) & (in_head < ROT)
 
-    def turn(block, b, sign):
+    def angles(b):
         cb, sb = cosb_ref[pl.ds(b, 1), :], sinb_ref[pl.ds(b, 1), :]
         cr, sr = cosr_ref[...], sinr_ref[...]
-        co = cr * cb - sr * sb
-        si = (sr * cb + cr * sb) * sign
-        co = jnp.where(in_head < ROT, co, 1.0)
-        up = pltpu.roll(block, 128 - ROT // 2, 1)
-        down = pltpu.roll(block, ROT // 2, 1)
-        mixed = jnp.where(first_rot, -up, down) * si
-        mixed = jnp.where(in_head < ROT, mixed, 0.0)
-        return block * co + mixed
-
-    ag_arrived(0, 1)
-    ag_start(0, 5)
-    ag_start(0, 3)
-    ag_arrived(0, 2)
-    ag_start(0, 6)
-    ag_start(0, 4)
-    for i in (1, 2, 0):
-        ag_start(1, i)
+        co = jnp.where(in_head < ROT, cr * cb - sr * sb, 1.0)
+        si = sr * cb + cr * sb
+        return co, jnp.where(first_rot, -si, 0.0), jnp.where(second_rot, si, 0.0)
+
+    def turn(block, table, back=False):
+        co, up, down = table
+        moved = pltpu.roll(block, 128 - ROT // 2, 1) * up + pltpu.roll(block, ROT // 2, 1) * down
+        return block * co - moved if back else block * co + moved
+
     norm_block(s)
     ag_arrived(0, 0)
     norm_block(peer(1))
+    own_dy.wait()
+    for i in (1, 2, 0):
+        ag_start(1, i)
     norm_block(peer(2))
+    norm_block(peer(4))
+    ag_arrived(0, 3)
+    norm_block(peer(3))
+    ag_arrived(0, 4)
+    norm_block(peer(5))
     ag_arrived(0, 6)
     ag_start(0, 7)
     ag_arrived(0, 5)
     ag_start(0, 8)
-    norm_block(peer(4))
-    z_forward(3)
-    ag_arrived(0, 3)
-    norm_block(peer(3))
-    ag_arrived(0, 4)
-    norm_block(peer(5))
     norm_block(peer(6))
     ag_arrived(0, 7)
     ag_arrived(0, 8)
@@ -618,192 +634,140 @@
     for m in range(1, 4):
         wo_copy(m, False).start()
     wout[pl.ds(aligned(32 * quad, 32), 32), :] = wz[quad]
-    z_forward(0)
-    z_send(2)
-    ag_arrived(1, 1)
-    ag_start(1, 5)
-    ag_start(1, 3)
-    ag_arrived(1, 2)
-    ag_start(1, 6)
-    ag_start(1, 4)
-    z_arrived(0)
+    z_arrived(0, paced=True)
 
     def qkv_step(b, carry):
         at = aligned(rows * b, rows)
         joined = dot(xn[pl.ds(at, rows), :], win[...])
-        q_s[pl.ds(at, rows), :] = turn(joined[:, :128], b, 1.0).astype(BF16) * jnp.asarray(HD**-0.5, BF16)
-        k_s[pl.ds(at, rows), :] = turn(joined[:, 128:256], b, 1.0).astype(BF16)
-        vx[pl.ds(at, rows), :128] = joined[:, 256:].astype(BF16)
-        vx[pl.ds(at, rows), 128:] = jnp.ones((rows, 128), BF16)
+        table = angles(b)
+        dfused[pl.ds(at, rows), :128] = (turn(joined[:, :128], table) * HD**-0.5).astype(BF16)
+        dfused[pl.ds(at, rows), 128:256] = turn(joined[:, 128:256], table).astype(BF16)
+        dfused[pl.ds(at, rows), 256:] = joined[:, 256:].astype(BF16)
         return carry
 
     lax.fori_loop(0, NP, qkv_step, 0)
-    KB = 2 * rows
+    QB = 2 * rows
+    lane_q = lax.broadcasted_iota(jnp.int32, (QB, 128), 1) < HD
 
     def wide(tile):
-        return jnp.concatenate([tile] * (KB // 128), axis=1)
+        return jnp.concatenate([tile] * (QB // 128), axis=1)
 
     def fold(v):
         out = v[:, :128]
-        for c in range(1, KB // 128):
+        for c in range(1, QB // 128):
             out = jnp.maximum(out, v[:, 128 * c : 128 * (c + 1)])
         return out
 
     def by_head(block):
         zero = jnp.zeros_like(block)
-        return jnp.where(low_head, block, zero), jnp.where(low_head, zero, block)
-
-    def hidden(i, j):
-        query = rows * i + lax.broadcasted_iota(jnp.int32, (rows, KB), 0)
-        key = KB * j + lax.broadcasted_iota(jnp.int32, (rows, KB), 1)
-        return key > query
+        return jnp.where(lane_q, block, zero), jnp.where(lane_q, zero, block)
+
+    def hidden():
+        return lax.broadcasted_iota(jnp.int32, (QB, QB), 1) > lax.broadcasted_iota(jnp.int32, (QB, QB), 0)
+
+    ones = jnp.ones((QB, 128), BF16)
 
     def attend_step(i, carry):
-        at = aligned(rows * i, rows)
-        last = lax.div(i, 2)
-        qh = by_head(q_s[pl.ds(at, rows), :])
-        kj = k_s[pl.ds(aligned(KB * last, KB), KB), :]
-        mask = hidden(i, last)
+        at = aligned(QB * i, QB)
+        qh = by_head(dfused[pl.ds(at, QB), :128])
+        kj = dfused[pl.ds(at, QB), 128:256]
+        mask = hidden()
         for h in range(2):
             sc = jnp.where(mask, masked_score, dot_nt(qh[h], kj))
-            sbuf[h, last] = sc
+            sbuf[h, i] = sc
             mref[h] = fold(sc)
 
         def scores(j, c2):
-            kk = k_s[pl.ds(aligned(KB * j, KB), KB), :]
+            kk = dfused[pl.ds(aligned(QB * j, QB), QB), 128:256]
             for h in range(2):
                 sc = dot_nt(qh[h], kk)
                 sbuf[h, j] = sc
                 mref[h] = jnp.maximum(mref[h], fold(sc))
             return c2
 
-        lax.fori_loop(0, last, scores, 0)
+        lax.fori_loop(0, i, scores, 0)
         for h in range(2):
-            mref[h] = jnp.broadcast_to(jnp.max(mref[h], axis=1, keepdims=True), (rows, 128))
-            acc[h] = jnp.zeros((rows, 256), F32)
+            mref[h] = jnp.broadcast_to(jnp.max(mref[h], axis=1, keepdims=True), (QB, 128))
+            acc[h] = jnp.zeros((QB, 256), F32)
 
         def weigh(j, c2):
-            vj = vx[pl.ds(aligned(KB * j, KB), KB), :]
+            vj = jnp.concatenate([dfused[pl.ds(aligned(QB * j, QB), QB), 256:], ones], axis=1)
             for h in range(2):
                 pj = jnp.exp(sbuf[h, j] - wide(mref[h])).astype(BF16)
                 acc[h] = acc[h] + dot(pj, vj)
             return c2
 
-        lax.fori_loop(0, last + 1, weigh, 0)
-        o_s[pl.ds(at, rows), :] = jnp.where(
-            low_head, acc[0][:, :128] / acc[0][:, 128:], acc[1][:, :128] / acc[1][:, 128:]
+        lax.fori_loop(0, i + 1, weigh, 0)
+        o_s[pl.ds(at, QB), :] = jnp.where(
+            lane_q, acc[0][:, :128] / acc[0][:, 128:], acc[1][:, :128] / acc[1][:, 128:]
         ).astype(BF16)
-        for h in range(2):
-            lse[h, pl.ds(at, rows), :] = mref[h] + jnp.log(acc[h][:, 128:])
-
-        @pl.when(i == 4)
+        lse[pl.ds(at, QB), :] = jnp.where(
+            lane_q, mref[0] + jnp.log(acc[0][:, 128:]), mref[1] + jnp.log(acc[1][:, 128:])
+        )
+
+        @pl.when(i == 1)
         def _():
-            z_forward(1)
+            z_forward(2)
+
+        @pl.when(i == 1)
+        def _():
+            ag_arrived(1, 1)
+            ag_start(1, 5)
+            ag_start(1, 3)
+            ag_arrived(1, 2)
+            ag_start(1, 6)
+            ag_start(1, 4)
         return carry
 
-    lax.fori_loop(0, NP, attend_step, 0)
+    lax.fori_loop(0, NP // 2, attend_step, 0)
+    z_forward(1)
     ag_arrived(1, 6)
     ag_start(1, 7)
     ag_arrived(1, 5)
     ag_start(1, 8)
+
     dkt[...] = jnp.zeros_like(dkt)
     dvt[...] = jnp.zeros_like(dvt)
 
     def attend_back(i):
-        at = aligned(rows * i, rows)
-        last = lax.div(i, 2)
-        qi = q_s[pl.ds(at, rows), :]
-        doi = do_s[pl.ds(at, rows), :]
+        at = aligned(QB * i, QB)
+        qi = dfused[pl.ds(at, QB), :128]
+        doi = do_s[pl.ds(at, QB), :]
         dof = doi.astype(F32)
         qh = by_head(qi)
         doh = by_head(doi)
         qt = jnp.transpose(qi.astype(F32)).astype(BF16)
         dot_t = jnp.transpose(dof).astype(BF16)
-        prod = dof * o_s[pl.ds(at, rows), :].astype(F32)
-        parts = by_head(prod)
+        parts = by_head(dof * o_s[pl.ds(at, QB), :].astype(F32))
         for h in range(2):
-            mref[h] = jnp.broadcast_to(jnp.sum(parts[h], axis=1, keepdims=True), (rows, 128))
-            dqacc[h] = jnp.zeros((rows, 128), F32)
+            mref[h] = jnp.broadcast_to(jnp.sum(parts[h], axis=1, keepdims=True), (QB, 128))
+            acc[h, :, :128] = jnp.broadcast_to(lse[pl.ds(at, QB), HD * h : HD * h + 1], (QB, 128))
+            acc[h, :, 128:] = jnp.zeros((QB, 128), F32)
 
         def unit(j, mask):
-            ja = aligned(KB * j, KB)
-            kk = k_s[pl.ds(ja, KB), :]
-            vj = vx[pl.ds(ja, KB), :128]
+            ja = aligned(QB * j, QB)
+            kk = dfused[pl.ds(ja, QB), 128:256]
+            vj = dfused[pl.ds(ja, QB), 256:]
             for h in range(2):
                 hs = slice(HD * h, HD * (h + 1))
-                p = jnp.exp(dot_nt(qh[h], kk) - wide(lse[h, pl.ds(at, rows), :]))
+                p = jnp.exp(dot_nt(qh[h], kk) - wide(acc[h, :, :128]))
                 if mask is not None:
                     p = jnp.where(mask, 0.0, p)
                 ds = (p * (dot_nt(doh[h], vj) - wide(mref[h]))).astype(BF16)
-                dqacc[h] = dqacc[h] + dot(ds, kk)
-                dkt[hs, pl.ds(ja, KB)] = dkt[hs, pl.ds(ja, KB)] + dot(qt[hs, :], ds)
-                dvt[hs, pl.ds(ja, KB)] = dvt[hs, pl.ds(ja, KB)] + dot(dot_t[hs, :], p.astype(BF16))
+                acc[h, :, 128:] = acc[h, :, 128:] + dot(ds, kk)
+                dkt[hs, pl.ds(ja, QB)] = dkt[hs, pl.ds(ja, QB)] + dot(qt[hs, :], ds)
+                dvt[hs, pl.ds(ja, QB)] = dvt[hs, pl.ds(ja, QB)] + dot(dot_t[hs, :], p.astype(BF16))
 
         def free(j, c2):
             unit(j, None)
             return c2
 
-        lax.fori_loop(0, last, free, 0)
-        unit(last, hidden(i, last))
-        dq = jnp.where(low_head, dqacc[0], dqacc[1]) * HD**-0.5
-        dfused[pl.ds(at, rows), :128] = turn(dq, i, -1.0).astype(BF16)
-
-    for i in (0, 3, 4, 7, 8):
-        ag_arrived(1, i)
-    for m in range(1, 4):
-        wo_copy(m, True).wait_recv()
-
-    def loop(n, f):
-        def step(i, carry):
-            f(i)
-            return carry
-        lax.fori_loop(0, n, step, 0)
-
-    def do_block(b):
-        at = aligned(rows * b, rows)
-        do_s[pl.ds(at, rows), :] = dot_nt(dyg[pl.ds(at, rows), :], wout[...]).astype(BF16)
-
-    loop(NP, do_block)
-    gout[...] = dot_tn(o_s[...], dyg[...]).astype(BF16)
-
-    def go_copy(m, incoming):
-        t4 = lax.rem(peer(m), 4)
-        src = gout.at[pl.ds(aligned(32 * t4, 32), 32)]
-        dst = gz.at[t4 if incoming else quad]
-        return rc(src, dst, go_s.at[m], go_r.at[m], d, peer(m))
-
-    for m in range(1, 4):
-        go_copy(m, False).start()
-    gz[quad] = gout[pl.ds(aligned(32 * quad, 32), 32), :]
-    early = 2
-
-    def back_early(step):
-        attend_back(NP - 1 - step)
-
-        @pl.when(step == 0)
-        def _():
-            z_forward(2)
-
-    loop(early, back_early)
-    z_arrived(1)
-    z_arrived(2)
-
-    eb = jnp.concatenate([vt[s, dd, 3:4, :] for dd in range(NZ)], axis=1)
-    geb[...] = jnp.zeros_like(geb)
-    sums[...] = jnp.zeros_like(sums)
-    sums[2:3, :] = jnp.sum(dy_ref[...].astype(F32), axis=0, keepdims=True)
-
-    def ffn_block(b):
-        at = aligned(rows * b, rows)
-        e = dot(xn[pl.ds(at, rows), :], wexp[...]) + eb
-        up = dot_nt(dyg[pl.ds(at, rows), :], wred[...])
-        a, slope = gelu_pair(e)
-        act_s[pl.ds(at, rows), :] = a.astype(BF16)
-        de = (up * slope).astype(BF16)
-        de_s[pl.ds(at, rows), :] = de
-        geb[...] = geb[...] + jnp.sum(de.astype(F32).reshape(rows // 8, 8, 4 * 128), axis=0)
-
-    loop(NP, ffn_block)
+        lax.fori_loop(0, i, free, 0)
+        unit(i, hidden())
+        for part in range(2):
+            piece = slice(rows * part, rows * (part + 1))
+            dq = jnp.where(low_head, acc[0, piece, 128:], acc[1, piece, 128:]) * HD**-0.5
+            dfused[pl.ds(aligned(at + rows * part, rows), rows), :128] = turn(dq, angles(2 * i + part), True).astype(BF16)
 
     GVIEW = (
         lambda b: gin.at[pl.ds(aligned(256 * b, 256), 256)],
@@ -883,14 +847,6 @@
             def _():
                 zr_copy(a, dest, dest, d, dest).wait_send()
 
-    def gexp_block(b):
-        at = aligned(256 * b, 256)
-        gexp[pl.ds(at, 256), :] = dot_tn(xn[:, pl.ds(at, 256)], de_s[...]).astype(BF16)
-
-    def gred_block(b):
-        at = aligned(128 * b, 128)
-        gred[pl.ds(at, 128), :] = dot_tn(act_s[:, pl.ds(at, 128)], dyg[...]).astype(BF16)
-
     def dest_send(a, dest):
         for src, via, to in COMB:
             if to == dest:
@@ -902,29 +858,96 @@
         def _():
             zr_copy(a, dest, dest, d, dest).start()
 
-    for dest in (3, 0, 2, 1):
-        gred_block(dest)
-        dest_send(2, dest)
+    for i in (0, 3, 4, 7, 8):
+        ag_arrived(1, i)
+    for m in range(1, 4):
+        wo_copy(m, True).wait_recv()
+
+    def loop(n, f):
+        def step(i, carry):
+            f(i)
+            return carry
+        lax.fori_loop(0, n, step, 0)
+
+    def do_block(b):
+        at = aligned(4 * rows * b, 4 * rows)
+        do_s[pl.ds(at, 4 * rows), :] = dot_nt(dyg[pl.ds(at, 4 * rows), :], wout[...]).astype(BF16)
+
+    loop(NP // 4, do_block)
+    gout[...] = dot_tn(o_s[...], dyg[...]).astype(BF16)
+
+    def go_copy(m, incoming):
+        t4 = lax.rem(peer(m), 4)
+        src = gout.at[pl.ds(aligned(32 * t4, 32), 32)]
+        dst = gz.at[t4 if incoming else quad]
+        return rc(src, dst, go_s.at[m], go_r.at[m], d, peer(m))
+
+    for m in range(1, 4):
+        go_copy(m, False).start()
+    gz[quad] = gout[pl.ds(aligned(32 * quad, 32), 32), :]
+    early = 1
+
+    def back_early(step):
+        attend_back(NP // 2 - 1 - step)
+
+    loop(early, back_early)
     for m in range(1, 4):
         go_copy(m, True).wait_recv()
     for dest in (3, 0, 2, 1):
         dest_send(3, dest)
+    z_arrived(1)
+    z_arrived(2)
+
+    for dd in range(NZ):
+        ebs[:, 128 * dd : 128 * (dd + 1)] = jnp.broadcast_to(vt[s, dd, 3:4, :], (8, 128))
+    geb[...] = jnp.zeros_like(geb)
+    sums[...] = jnp.zeros_like(sums)
+    sums[2:3, :] = jnp.sum(dyg[pl.ds(aligned(rows * s, rows), rows), :].astype(F32), axis=0, keepdims=True)
+
+    def ffn_block(b):
+        at = pl.ds(aligned(rows * b, rows), rows)
+        e = dot(xn[at, :], wexp[...]) + ebs[0:1, :]
+        up = dot_nt(dyg[at, :], wred[...])
+        a, slope = gelu_pair(e)
+        act_s[at, :] = a.astype(BF16)
+        de = (up * slope).astype(BF16)
+        de_s[at, :] = de
+        geb[...] = geb[...] + jnp.sum(de.astype(F32).reshape(rows // 8, 8, 4 * 128), axis=0)
+
+    loop(NP, ffn_block)
+
+    def gexp_block(b):
+        at = aligned(256 * b, 256)
+        gexp[pl.ds(at, 256), :] = dot_tn(xn[:, pl.ds(at, 256)], de_s[...]).astype(BF16)
+
+    def gred_block(b):
+        at = aligned(128 * b, 128)
+        gred[pl.ds(at, 128), :] = dot_tn(act_s[:, pl.ds(at, 128)], dyg[...]).astype(BF16)
+
+    for dest in (3, 0, 2, 1):
+        gred_block(dest)
+        dest_send(2, dest)
 
     for i in range(9):
         ag_copy(0, i, False).wait_send()
 
-    def out_block(b):
-        at = aligned(rows * b, rows)
-        pout[pl.ds(at, rows), :] = (
-            dot(o_s[pl.ds(at, rows), :], wout[...]) + dot(act_s[pl.ds(at, rows), :], wred[...])
-        ).astype(BF16)
-
-    def dn_block(b):
-        at = aligned(rows * b, rows)
-        dn = dot_nt(de_s[pl.ds(at, rows), :], wexp[...]) + dot_nt(dfused[pl.ds(at, rows), :], win[...])
-        pdn[pl.ds(at, rows), :] = dn.astype(BF16)
-        sums[0:1, :] = sums[0:1, :] + jnp.sum(dn * xn[pl.ds(at, rows), :].astype(F32), axis=0, keepdims=True)
-        sums[1:2, :] = sums[1:2, :] + jnp.sum(dn, axis=0, keepdims=True)
+    def chip_rows(m):
+        return aligned(2 * rows * lax.div(peer(m), 2), 2 * rows)
+
+    def out_block(m):
+        at = pl.ds(chip_rows(m), 2 * rows)
+        for c in range(0, D, D // 2):
+            cols = slice(c, c + D // 2)
+            pout[at, cols] = (dot(o_s[at, :], wout[:, cols]) + dot(act_s[at, :], wred[:, cols])).astype(BF16)
+
+    def dn_block(m):
+        at = pl.ds(chip_rows(m), 2 * rows)
+        for c in range(0, D, D // 2):
+            cols = slice(c, c + D // 2)
+            dn = dot_nt(de_s[at, :], wexp[cols, :]) + dot_nt(dfused[at, :], win[cols, :])
+            pdn[at, cols] = dn.astype(BF16)
+            sums[0:1, cols] = sums[0:1, cols] + jnp.sum(dn * xn[at, cols].astype(F32), axis=0, keepdims=True)
+            sums[1:2, cols] = sums[1:2, cols] + jnp.sum(dn, axis=0, keepdims=True)
 
     RS = ((pout, sib_o, r1_o, r2_o), (pdn, sib_d, r1_d, r2_d))
 
@@ -938,8 +961,10 @@
         (1, 1, 0, rows, lambda w: RS[w][1].at[3]),
         (2, 6, 0, half, lambda w: RS[w][2].at[0]),
         (4, 6, half, half, lambda w: RS[w][2].at[1]),
-        (2, 2, 0, rows, lambda w: RS[w][3].at[0]),
-        (4, 4, 0, rows, lambda w: RS[w][3].at[1]),
+        (2, 2, 0, half, lambda w: RS[w][3].at[0, pl.ds(0, half)]),
+        (4, 4, half, half, lambda w: RS[w][3].at[1, pl.ds(half, half)]),
+        (2, 2, half, half, lambda w: RS[w][3].at[0, pl.ds(half, half)]),
+        (4, 4, 0, half, lambda w: RS[w][3].at[1, pl.ds(0, half)]),
     )
 
     def rs_copy(w, i):
@@ -961,52 +986,54 @@
     def rs_pair(w, which):
         rs_copy(w, 1 + which).wait_recv()
         add_into(w, (2, 4)[which], 0, rows, RS[w][1].at[1 + which])
+        rs_copy(w, 6 + which).start()
 
     def rs_near(w, which):
         rs_copy(w, 5 - which).wait_recv()
         add_into(w, (2, 4)[which], (half, 0)[which], half, RS[w][2].at[1 - which])
-        rs_copy(w, 6 + which).start()
+        rs_copy(w, 8 + which).start()
 
     def rs_last(w):
-        for i in (3, 6, 7):
+        for i in (3, 6, 7, 8, 9):
             rs_copy(w, i).wait_recv()
 
-    for i, m in enumerate((7, 3, 5, 1)):
-        out_block(peer(m))
+    for i, m in enumerate((7, 3)):
+        out_block(m)
         rs_copy(0, i).start()
     for dest in (3, 0, 2, 1):
         gexp_block(dest)
         dest_send(1, dest)
-    for m in (6, 2, 4, 0):
-        out_block(peer(m))
-
-    def back_late(step):
-        attend_back(NP - 1 - early - step)
+    for i, m in ((2, 5), (3, 1)):
+        out_block(m)
+        rs_copy(0, i).start()
+
+    def back_step(step):
+        attend_back(NP // 2 - 1 - early - step)
 
         @pl.when(step == 0)
         def _():
             rs_across(0)
             zr_join(2)
+            rs_pair(0, 0)
+            rs_pair(0, 1)
 
         @pl.when(step == 1)
         def _():
-            rs_pair(0, 0)
-            rs_pair(0, 1)
             zr_join(3)
+            rs_near(0, 0)
+            rs_near(0, 1)
 
         @pl.when(step == 2)
         def _():
-            rs_near(0, 0)
-            rs_near(0, 1)
             zr_join(1)
 
-    loop(NP - early, back_late)
+    loop(NP // 2 - early, back_step)
 
     def kv_block(b):
         at = aligned(rows * b, rows)
         dk = jnp.transpose(dkt[:, pl.ds(at, rows)])
         dv = jnp.transpose(dvt[:, pl.ds(at, rows)])
-        dfused[pl.ds(at, rows), 128:256] = turn(dk, b, -1.0).astype(BF16)
+        dfused[pl.ds(at, rows), 128:256] = turn(dk, angles(b), True).astype(BF16)
         dfused[pl.ds(at, rows), 256:] = dv.astype(BF16)
 
     loop(NP, kv_block)
@@ -1015,25 +1042,11 @@
         at = aligned(256 * b, 256)
         gin[pl.ds(at, 256), :] = dot_tn(xn[:, pl.ds(at, 256)], dfused[...]).astype(BF16)
 
-    for dest in (3, 0):
-        gin_block(dest)
-        dest_send(0, dest)
-    dn_block(peer(7))
-    rs_copy(1, 0).start()
-    for dest in (2, 1):
-        gin_block(dest)
-        dest_send(0, dest)
-    for i, m in ((1, 3), (2, 5), (3, 1)):
-        dn_block(peer(m))
+    for i, m in enumerate((7, 3, 5)):
+        dn_block(m)
         rs_copy(1, i).start()
-    zr_join(0)
-    dn_block(peer(6))
     rs_across(1)
-    dn_block(peer(2))
-    rs_pair(1, 0)
-    dn_block(peer(4))
-    rs_pair(1, 1)
-    dn_block(s)
+    dn_block(1)
     for yy in range(2):
         for dd in range(NZ):
             group = 2 * dd + yy
@@ -1044,8 +1057,30 @@
 
     for m in range(1, NP):
         sp_copy(m).start()
-
+    rs_copy(1, 3).start()
+    rs_pair(1, 0)
+    rs_pair(1, 1)
+    for dest in (3, 0, 2, 1):
+        gin_block(dest)
+        dest_send(0, dest)
+    rs_near(1, 0)
+    rs_near(1, 1)
+    zr_join(0)
     geb_row = jnp.sum(geb[...], axis=0, keepdims=True)
+    for m in range(1, NP):
+        sp_copy(m).wait_recv()
+    tiles = sv[ybit]
+    for m in range(1, NP):
+        tiles = tiles + rv[m]
+    for dd in range(NZ):
+        ebt = jnp.broadcast_to(geb_row[:, 128 * dd : 128 * (dd + 1)], (8, 128))
+        zt[dd] = jnp.where(rows8 == 3, ebt, tiles[dd])
+
+    def sz_copy(i, incoming):
+        return rc(zt.at[other(i)], rzv.at[i], sz_s.at[i], sz_r.at[i], other(i), s)
+
+    for i in range(1, NZ):
+        sz_copy(i, False).start()
 
     def total_rows(a, n):
         ref, use = zr_total(a)
@@ -1064,8 +1099,6 @@
     total_rows(1, 256)
     for m in range(1, NP):
         back_copy(1, m, False).start()
-    rs_near(1, 0)
-    rs_near(1, 1)
 
     ref_r, use_r = zr_total(2)
 
@@ -1093,27 +1126,13 @@
         at = aligned(32 * c, 32)
         dn = rs_total32(1, c)
         unit, inv = unit_of(x_ref[pl.ds(at, 32), :])
-        dyf = dy_ref[pl.ds(at, 32), :].astype(F32)
+        dyf = dyg[pl.ds(aligned(rows * s + 32 * c, 32), 32), :].astype(F32)
         g = dn * vecs[0:1, :]
         hg = inv * (
             g - jnp.mean(g, axis=1, keepdims=True) - unit * jnp.mean(g * unit, axis=1, keepdims=True)
         ) + dyf
         hgrad_ref[pl.ds(at, 32), :] = hg.astype(BF16)
 
-    for m in range(1, NP):
-        sp_copy(m).wait_recv()
-    tiles = sv[ybit]
-    for m in range(1, NP):
-        tiles = tiles + rv[m]
-    for dd in range(NZ):
-        ebt = jnp.broadcast_to(geb_row[:, 128 * dd : 128 * (dd + 1)], (8, 128))
-        zt[dd] = jnp.where(rows8 == 3, ebt, tiles[dd])
-
-    def sz_copy(i, incoming):
-        return rc(zt.at[other(i)], rzv.at[i], sz_s.at[i], sz_r.at[i], other(i), s)
-
-    for i in range(1, NZ):
-        sz_copy(i, False).start()
     total_rows(0, 256)
     for m in range(1, NP):
         back_copy(0, m, False).start()
@@ -1154,7 +1173,7 @@
     for i in range(9):
         ag_copy(1, i, False).wait_send()
     for w in range(2):
-        for i in range(8):
+        for i in range(10):
             rs_copy(w, i).wait_send()
     for a in range(4):
         z_sent(a)
@@ -1229,22 +1248,22 @@
         vm((seq, D), BF16), vm((seq, D), BF16), vm((seq, D), BF16),
         vm((D, 384), BF16), vm((D, ff), BF16), vm((ff, D), BF16), vm((128, D), BF16), vm((NZ, 32, D), BF16),
         vm((NP, 32, 384), BF16), vm((NP, 32, ff), BF16),
-        vm((seq, 128), BF16), vm((seq, 128), BF16), vm((seq, 256), BF16), vm((seq, 128), BF16), vm((seq, 128), BF16),
+        vm((seq, 128), BF16), vm((seq, 128), BF16),
         vm((128, seq), F32), vm((128, seq), F32), vm((seq, 384), BF16),
-        vm((2, NP // 2, rows, 2 * rows), F32), vm((2, seq, 128), F32),
-        vm((2, rows, 128), F32), vm((2, rows, 256), F32), vm((2, rows, 128), F32),
+        vm((2, NP // 2, 2 * rows, 2 * rows), F32), vm((seq, 128), F32),
+        vm((2, 2 * rows, 128), F32), vm((2, 2 * rows, 256), F32),
         vm((seq, ff), BF16), vm((seq, ff), BF16), vm((seq, D), BF16),
         vm((4, rows, D), BF16), vm((4, rows, D), BF16),
         vm((2, rows // 2, D), BF16), vm((2, rows, D), BF16), vm((2, rows // 2, D), BF16), vm((2, rows, D), BF16),
         vm((D, 384), BF16), vm((D, ff), BF16), vm((ff, D), BF16), vm((128, D), BF16), vm((NZ, 32, D), BF16),
         vm((NZ, 256, 384), BF16), vm((NZ, 256, ff), BF16), vm((NZ, 128, D), BF16), vm((NZ, 32, D), BF16),
         vm((NP, 32, 384), BF16), vm((NP, 32, ff), BF16),
-        vm((NP, NZ, 8, 128), F32), vm((8, D), F32), vm((8, ff), F32), vm((8, D), F32),
+        vm((NP, NZ, 8, 128), F32), vm((8, D), F32), vm((8, ff), F32), vm((8, ff), F32), vm((8, D), F32),
         vm((2, NZ, 8, 128), F32), vm((NP, NZ, 8, 128), F32), vm((NZ, 8, 128), F32), vm((NZ, 8, 128), F32),
         dma((2, NP)), dma((2, NP)), dma((2, 9)), dma((2, 9)), dma((4, 5)), dma((4, 4)),
         dma((NZ,)), dma((NZ,)), dma((NP,)), dma((NP,)), dma((4,)), dma((4,)),
-        dma((2, 8)), dma((2, 8)), dma((4, 4)), dma((4, 4)), dma((4,)), dma((4,)),
-        dma((2, NP)), dma((2, NP)), dma((NP,)), dma((NP,)), dma((NZ,)), dma((NZ,)),
+        dma((2, 10)), dma((2, 10)), dma((4, 4)), dma((4, 4)), dma((4,)), dma((4,)),
+        dma((2, NP)), dma((2, NP)), dma((NP,)), dma((NP,)), dma((NZ,)), dma((NZ,)), dma,
     ]
     in_vmem = pl.BlockSpec(memory_space=pltpu.VMEM)
     in_smem = pl.BlockSpec(memory_space=pltpu.SMEM)
@@ -1261,7 +1280,7 @@
             jax.ShapeDtypeStruct((128, D), F32), jax.ShapeDtypeStruct((32, D), F32),
             jax.ShapeDtypeStruct((8, 128), F32),
         ],
-        in_specs=[in_vmem] * 14,
+        in_specs=[in_vmem, pl.BlockSpec(memory_space=pl.ANY)] + [in_vmem] * 12,
         out_specs=[in_vmem] * 7,
         scratch_shapes=scratch,
         compiler_params=pltpu.CompilerParams(

time: 169 us -> 138 us (0.82); the launches traced: 169 us -> 135 us
  Pallas kernels: 167 us -> 133 us
    pallas_call x1, Pallas kernels: 161 us -> 128 us  [fused_shards(): pl.pallas_call(body, out_shape=[rows_shape, rows_shape, jax.ShapeDtypeStr...]
where the time goes in v3:
time: 138 us; the launch traced here: 135 us
  Pallas kernels  133 us (96%)
  between operations  2.13 us (2%)
    pallas_call x1, Pallas kernels, fused_shards(): pl.pallas_call(body, out_shape=[rows_shape, rows_shape, jax.ShapeDtypeStr...  128 us
    pallas_call x1, Pallas kernels, fused_shards(): pl.pallas_call(update_kernel, out_shape=[rows_shape, rows_shape] + shard_...  5.19 us

profile of v3, /device:TPU:13, one launch (start us, length us, event | category | flops | bytes accessed | tf_op | source)
XLA Modules:
  0.0 135.1 jit_solution(14794729864364512752)
XLA Ops:
  1.9 127.8 %block_step.1 = (bf16[256,1024]{1,0:T(8,128)(2,1)}, bf16[256,1024]{1,0:T(8,128)(2,1)}, bf16[8,32,384]{2,1,0:T(8,128)(2,1)}, bf16[8,32,512]{2,1,0:T(8,128)(2,1)},...) custom-call(bf16[256,1024]{1,0:T(8,128)(2,1)} %bitcast.20, bf16[256,1024]{1,0:T(8,128)(2,1)} %bitcast.21, ...), custom_call_target="tpu_custom_call" | custom-call | tf_op jit(solution)/shard_map/block_step/pallas_call | solution.py:1275
  129.7 5.2 %block_update.1 = (bf16[256,1024]{1,0:T(8,128)(2,1)}, bf16[256,1024]{1,0:T(8,128)(2,1)}, f32[1,32]{1,0:T(1,128)}, f32[1,32]{1,0:T(1,128)}, f32[32,3072]{1,0:T(8,...) custom-call(f32[1,32]{1,0:T(1,128)} %bitcast.23, ...), custom_call_target="tpu_custom_call" | custom-call | tf_op jit(solution)/shard_map/block_update/pallas_call | solution.py:1293

commit v4 on v3

--- a/solution.py
+++ b/solution.py
@@ -338,7 +338,7 @@
     (
         x_ref, dy_ref, gain_ref, shift_ref, win_ref, wout_ref, wexp_ref, ebias_ref, wred_ref, rbias_ref,
         cosr_ref, sinr_ref, cosb_ref, sinb_ref,
-        hout_ref, hgrad_ref, ra_in, ra_exp, tred_ref, tout_ref, tile_ref,
+        hout_out, hgrad_out, in_out, exp_out, tred_out, tout_out, tile_ref,
         xg, dyg, xn, win, wexp, wred, wout, wz, pin, pexp,
         o_s, do_s, dkt, dvt, dfused, sbuf, lse, mref, acc,
         act_s, de_s, pdn, sib_o, sib_d, r1_o, r2_o, r1_d, r2_d,
@@ -346,6 +346,7 @@
         vt, vecs, ebs, geb, sums, sv, rv, zt, rzv,
         a2a_s, a2a_r, ag_s, ag_r, z_s, z_r, vz_s, vz_r, vp_s, vp_r, wo_s, wo_r,
         rs_s, rs_r, zr_s, zr_r, go_s, go_r, b_s, b_r, sp_s, sp_r, sz_s, sz_r, dy_sem,
+        hout_ref, hgrad_ref, tred_ref, tout_ref, out_sem,
     ) = refs
     pout = xg
     d = lax.axis_index("dp")
@@ -423,14 +424,16 @@
     pack_in()
     pl.semaphore_wait(barrier, NP - 1 + NZ - 1)
 
+    def bundle(ref, ssem, rsem):
+        return rc(ref, ref, ssem, rsem, d, peer(1))
+
     def a2a_msg(which, m):
         src = (pin, pexp)[which].at[m]
         dst = (win, wexp)[which].at[pl.ds(own_rows, 32)]
-        return rc(src, dst, a2a_s.at[which, m], a2a_r.at[which, m], d, peer(m))
-
-    def a2a_arrived(which, m):
-        dst = (win, wexp)[which].at[pl.ds(aligned(32 * (8 * d + peer(m)), 32), 32)]
-        rc((pin, pexp)[which].at[m], dst, a2a_s.at[which, m], a2a_r.at[which, m], d, peer(m)).wait_recv()
+        return rc(src, dst, a2a_s.at[which], a2a_r.at[which], d, peer(m))
+
+    def a2a_group(which):
+        return bundle((pin, pexp)[which].at[pl.ds(1, NP - 1)], a2a_s.at[which], a2a_r.at[which])
 
     half = rows // 2
     AG = (
@@ -444,7 +447,10 @@
         buf = (xg, dyg)[which]
         at = rows * peer(blk ^ (to if incoming else 0)) + lo
         ref = buf.at[pl.ds(aligned(at, half), n)]
-        return rc(ref, ref, ag_s.at[which, i], ag_r.at[which, i], d, peer(to))
+        return rc(ref, ref, ag_s.at[which], ag_r.at[which, i], d, peer(to))
+
+    def ag_sent(which):
+        bundle((xg, dyg)[which].at[pl.ds(0, 7 * rows)], ag_s.at[which], ag_r.at[which, 0]).wait_send()
 
     def ag_start(which, i):
         ag_copy(which, i, False).start()
@@ -471,19 +477,19 @@
         for dest in (3, 0, 2, 1):
             @pl.when(z_direct(dest))
             def _():
-                rc(ZVIEW[a](d), ZVIEW[a](d), z_s.at[a, dest], z_r.at[a, d], dest, s).start()
+                rc(ZVIEW[a](d), ZVIEW[a](d), z_s.at[a], z_r.at[a, d], dest, s).start()
 
     FWD = ((2, 0, 3), (1, 3, 0))
 
     def z_wait_block(a, b):
-        rc(ZVIEW[a](b), ZVIEW[a](b), z_s.at[a, 4], z_r.at[a, b], d, s).wait_recv()
+        rc(ZVIEW[a](b), ZVIEW[a](b), z_s.at[a], z_r.at[a, b], d, s).wait_recv()
 
     def z_forward(a):
         for at, blk, dest in FWD:
             @pl.when(d == at)
             def _():
                 z_wait_block(a, blk)
-                rc(ZVIEW[a](blk), ZVIEW[a](blk), z_s.at[a, 4], z_r.at[a, blk], dest, s).start()
+                rc(ZVIEW[a](blk), ZVIEW[a](blk), z_s.at[a], z_r.at[a, blk], dest, s).start()
 
     PACE = ((0, 1), (3, 2))
 
@@ -508,25 +514,27 @@
                 z_wait_block(a, b)
 
     def z_sent(a):
-        for dest in range(NZ):
-            @pl.when(z_direct(dest))
-            def _():
-                rc(ZVIEW[a](d), ZVIEW[a](d), z_s.at[a, dest], z_r.at[a, d], dest, s).wait_send()
-        for at, blk, dest in FWD:
-            @pl.when(d == at)
-            def _():
-                rc(ZVIEW[a](blk), ZVIEW[a](blk), z_s.at[a, 4], z_r.at[a, blk], dest, s).wait_send()
+        whole = (win, wexp, wred, wz)[a]
+        inner = (d == 1) | (d == 2)
+
+        @pl.when(inner)
+        def _():
+            bundle(whole, z_s.at[a], z_r.at[a, 0]).wait_send()
+
+        @pl.when(jnp.logical_not(inner))
+        def _():
+            bundle(whole.at[pl.ds(0, whole.shape[0] // 2)], z_s.at[a], z_r.at[a, 0]).wait_send()
 
     def other(i):
         return lax.rem(d + i, NZ)
 
     def vz_copy(i, incoming):
         b = lax.rem(d + NZ - i, NZ) if incoming else d
-        return rc(vt.at[s, b], vt.at[s, b], vz_s.at[i], vz_r.at[i], other(i), s)
+        return rc(vt.at[s, b], vt.at[s, b], vz_s.at[0], vz_r.at[0], other(i), s)
 
     def vp_copy(m, incoming):
         b = peer(m) if incoming else s
-        return rc(vt.at[b], vt.at[b], vp_s.at[m], vp_r.at[m], d, peer(m))
+        return rc(vt.at[b], vt.at[b], vp_s.at[0], vp_r.at[0], d, peer(m))
 
     for i in range(1, NZ):
         vz_copy(i, False).start()
@@ -537,12 +545,11 @@
         ag_start(0, i)
     pack_exp()
     wred[pl.ds(aligned(128 * d, 128), 128), :] = wred_ref[...].astype(BF16)
-    for i in range(1, NZ):
-        vz_copy(i, True).wait_recv()
+    vz_group = bundle(zt.at[pl.ds(1, NZ - 1)], vz_s.at[0], vz_r.at[0])
+    vz_group.wait_recv()
     for m in range(1, NP):
         vp_copy(m, False).start()
-    for m in range(1, NP):
-        a2a_arrived(0, m)
+    a2a_group(0).wait_recv()
     z_send(0)
     for m in range(1, NP):
         a2a_msg(1, m).start()
@@ -556,18 +563,17 @@
     ag_arrived(0, 2)
     ag_start(0, 6)
     ag_start(0, 4)
-    for m in range(1, NP):
-        a2a_arrived(1, m)
+    a2a_group(1).wait_recv()
     z_send(1)
 
     def wo_copy(m, incoming):
         src = wz.at[lax.rem(peer(m), 4)]
         r = lax.rem(peer(m), 4) if incoming else quad
         dst = wout.at[pl.ds(aligned(32 * r, 32), 32)]
-        return rc(src, dst, wo_s.at[m], wo_r.at[m], d, peer(m))
-
-    for m in range(1, NP):
-        vp_copy(m, True).wait_recv()
+        return rc(src, dst, wo_s.at[0], wo_r.at[0], d, peer(m))
+
+    vp_group = bundle(rv.at[pl.ds(1, NP - 1)], vp_s.at[0], vp_r.at[0])
+    vp_group.wait_recv()
     for dd in range(NZ):
         for yy in range(2):
             group = 2 * dd + yy
@@ -636,16 +642,19 @@
     wout[pl.ds(aligned(32 * quad, 32), 32), :] = wz[quad]
     z_arrived(0, paced=True)
 
-    def qkv_step(b, carry):
-        at = aligned(rows * b, rows)
-        joined = dot(xn[pl.ds(at, rows), :], win[...])
-        table = angles(b)
-        dfused[pl.ds(at, rows), :128] = (turn(joined[:, :128], table) * HD**-0.5).astype(BF16)
-        dfused[pl.ds(at, rows), 128:256] = turn(joined[:, 128:256], table).astype(BF16)
-        dfused[pl.ds(at, rows), 256:] = joined[:, 256:].astype(BF16)
+    def qkv_step(n, carry):
+        joined = dot(xn[pl.ds(aligned(2 * rows * n, 2 * rows), 2 * rows), :], win[...])
+        for part in range(2):
+            b = 2 * n + part
+            at = pl.ds(aligned(rows * b, rows), rows)
+            piece = joined[rows * part : rows * (part + 1)]
+            table = angles(b)
+            dfused[at, :128] = (turn(piece[:, :128], table) * HD**-0.5).astype(BF16)
+            dfused[at, 128:256] = turn(piece[:, 128:256], table).astype(BF16)
+            dfused[at, 256:] = piece[:, 256:].astype(BF16)
         return carry
 
-    lax.fori_loop(0, NP, qkv_step, 0)
+    lax.fori_loop(0, NP // 2, qkv_step, 0)
     QB = 2 * rows
     lane_q = lax.broadcasted_iota(jnp.int32, (QB, 128), 1) < HD
 
@@ -787,7 +796,7 @@
         return ok
 
     def zr_copy(a, src_block, dest, slot, sem):
-        return rc(GVIEW[a](src_block), RZ[a].at[slot], zr_s.at[a, sem], zr_r.at[a, slot], dest, s)
+        return rc(GVIEW[a](src_block), RZ[a].at[slot], zr_s.at[a], zr_r.at[a, slot], dest, s)
 
     def zr_first(a):
         for src, via, dest in COMB:
@@ -840,12 +849,8 @@
         return total
 
     def zr_sent(a):
-        for dest in range(NZ):
-            sent = d != dest
-
-            @pl.when(sent)
-            def _():
-                zr_copy(a, dest, dest, d, dest).wait_send()
+        whole = (gin, gexp, gred, gz)[a]
+        bundle(whole.at[pl.ds(0, whole.shape[0] // 4 * 3)], zr_s.at[a], zr_r.at[a, 0]).wait_send()
 
     def dest_send(a, dest):
         for src, via, to in COMB:
@@ -860,8 +865,8 @@
 
     for i in (0, 3, 4, 7, 8):
         ag_arrived(1, i)
-    for m in range(1, 4):
-        wo_copy(m, True).wait_recv()
+    wo_group = bundle(wz.at[pl.ds(1, 3)], wo_s.at[0], wo_r.at[0])
+    wo_group.wait_recv()
 
     def loop(n, f):
         def step(i, carry):
@@ -880,7 +885,7 @@
         t4 = lax.rem(peer(m), 4)
         src = gout.at[pl.ds(aligned(32 * t4, 32), 32)]
         dst = gz.at[t4 if incoming else quad]
-        return rc(src, dst, go_s.at[m], go_r.at[m], d, peer(m))
+        return rc(src, dst, go_s.at[0], go_r.at[0], d, peer(m))
 
     for m in range(1, 4):
         go_copy(m, False).start()
@@ -891,8 +896,8 @@
         attend_back(NP // 2 - 1 - step)
 
     loop(early, back_early)
-    for m in range(1, 4):
-        go_copy(m, True).wait_recv()
+    go_group = bundle(gz.at[pl.ds(1, 3)], go_s.at[0], go_r.at[0])
+    go_group.wait_recv()
     for dest in (3, 0, 2, 1):
         dest_send(3, dest)
     z_arrived(1)
@@ -920,16 +925,20 @@
         at = aligned(256 * b, 256)
         gexp[pl.ds(at, 256), :] = dot_tn(xn[:, pl.ds(at, 256)], de_s[...]).astype(BF16)
 
-    def gred_block(b):
-        at = aligned(128 * b, 128)
-        gred[pl.ds(at, 128), :] = dot_tn(act_s[:, pl.ds(at, 128)], dyg[...]).astype(BF16)
-
-    for dest in (3, 0, 2, 1):
-        gred_block(dest)
-        dest_send(2, dest)
-
-    for i in range(9):
-        ag_copy(0, i, False).wait_send()
+    def gred_pair(one, two):
+        left = jnp.concatenate(
+            [act_s[:, 128 * one : 128 * (one + 1)], act_s[:, 128 * two : 128 * (two + 1)]], axis=1
+        )
+        both = dot_tn(left, dyg[...]).astype(BF16)
+        gred[128 * one : 128 * (one + 1), :] = both[:128]
+        gred[128 * two : 128 * (two + 1), :] = both[128:]
+
+    for pair in ((3, 0), (2, 1)):
+        gred_pair(*pair)
+        for dest in pair:
+            dest_send(2, dest)
+
+    ag_sent(0)
 
     def chip_rows(m):
         return aligned(2 * rows * lax.div(peer(m), 2), 2 * rows)
@@ -969,7 +978,7 @@
 
     def rs_copy(w, i):
         to, blk, lo, n, land = RSM[i]
-        return rc(part(w, blk, lo, n), land(w), rs_s.at[w, i], rs_r.at[w, i], d, peer(to))
+        return rc(part(w, blk, lo, n), land(w), rs_s.at[w], rs_r.at[w, i], d, peer(to))
 
     def add_into(w, m, lo, n, came):
         def step(c):
@@ -1032,9 +1041,9 @@
     def kv_block(b):
         at = aligned(rows * b, rows)
         dk = jnp.transpose(dkt[:, pl.ds(at, rows)])
-        dv = jnp.transpose(dvt[:, pl.ds(at, rows)])
+        dv = jnp.transpose(dvt[:, pl.ds(at, rows)].astype(BF16))
         dfused[pl.ds(at, rows), 128:256] = turn(dk, angles(b), True).astype(BF16)
-        dfused[pl.ds(at, rows), 256:] = dv.astype(BF16)
+        dfused[pl.ds(at, rows), 256:] = dv
 
     loop(NP, kv_block)
 
@@ -1046,29 +1055,32 @@
         dn_block(m)
         rs_copy(1, i).start()
     rs_across(1)
+    for dest in (3, 0):
+        gin_block(dest)
+        dest_send(0, dest)
     dn_block(1)
+    rs_copy(1, 3).start()
     for yy in range(2):
         for dd in range(NZ):
             group = 2 * dd + yy
             sv[yy, dd] = sums[:, 128 * group : 128 * (group + 1)]
 
     def sp_copy(m):
-        return rc(sv.at[lax.div(peer(m), 4)], rv.at[m], sp_s.at[m], sp_r.at[m], d, peer(m))
+        return rc(sv.at[lax.div(peer(m), 4)], rv.at[m], sp_s.at[0], sp_r.at[0], d, peer(m))
 
     for m in range(1, NP):
         sp_copy(m).start()
-    rs_copy(1, 3).start()
     rs_pair(1, 0)
     rs_pair(1, 1)
-    for dest in (3, 0, 2, 1):
+    for dest in (2, 1):
         gin_block(dest)
         dest_send(0, dest)
+    zr_join(0)
     rs_near(1, 0)
     rs_near(1, 1)
-    zr_join(0)
     geb_row = jnp.sum(geb[...], axis=0, keepdims=True)
-    for m in range(1, NP):
-        sp_copy(m).wait_recv()
+    sp_group = bundle(rv.at[pl.ds(1, NP - 1)], sp_s.at[0], sp_r.at[0])
+    sp_group.wait_recv()
     tiles = sv[ybit]
     for m in range(1, NP):
         tiles = tiles + rv[m]
@@ -1077,7 +1089,7 @@
         zt[dd] = jnp.where(rows8 == 3, ebt, tiles[dd])
 
     def sz_copy(i, incoming):
-        return rc(zt.at[other(i)], rzv.at[i], sz_s.at[i], sz_r.at[i], other(i), s)
+        return rc(zt.at[other(i)], rzv.at[i], sz_s.at[0], sz_r.at[0], other(i), s)
 
     for i in range(1, NZ):
         sz_copy(i, False).start()
@@ -1094,7 +1106,10 @@
     def back_copy(which, m, incoming):
         src = (gin, gexp)[which].at[pl.ds(aligned(256 * d + 32 * peer(m), 32), 32)]
         dst = (rb_in, rb_exp)[which].at[m]
-        return rc(src, dst, b_s.at[which, m], b_r.at[which, m], d, peer(m))
+        return rc(src, dst, b_s.at[which], b_r.at[which], d, peer(m))
+
+    def back_group(which):
+        return bundle((rb_in, rb_exp)[which].at[pl.ds(1, NP - 1)], b_s.at[which], b_r.at[which])
 
     total_rows(1, 256)
     for m in range(1, NP):
@@ -1106,6 +1121,16 @@
         at = aligned(32 * c, 32)
         tred_ref[pl.ds(at, 32), :] = zr_sum(2, use_r, ref_r[pl.ds(at, 32), :].astype(F32), at, 32)
     loop(4, red_total)
+    mine = pl.ds(aligned(256 * d + 32 * s, 32), 32)
+    leaving = []
+
+    def leave(src, dst):
+        out = pltpu.make_async_copy(src, dst, out_sem.at[len(leaving)])
+        out.start()
+        leaving.append(out)
+
+    leave(tred_ref, tred_out)
+    leave(gexp.at[mine], exp_out.at[0])
     rs_last(0)
 
     def out_final(c):
@@ -1122,6 +1147,7 @@
         return own + RS[w][3][1, pl.ds(at, 32), :].astype(F32)
 
     loop(rows // 32, out_final)
+    leave(hout_ref, hout_out)
     def grad_final(c):
         at = aligned(32 * c, 32)
         dn = rs_total32(1, c)
@@ -1137,44 +1163,34 @@
     for m in range(1, NP):
         back_copy(0, m, False).start()
     rs_last(1)
+    leave(gin.at[mine], in_out.at[0])
     loop(rows // 32, grad_final)
+    leave(hgrad_ref, hgrad_out)
     ref_o, use_o = zr_total(3)
     tout_ref[...] = zr_sum(3, use_o, ref_o[...].astype(F32), 0, 32)
 
-    mine = pl.ds(aligned(256 * d + 32 * s, 32), 32)
-    ra_exp[0] = gexp[mine, :]
-    ra_in[0] = gin[mine, :]
-    for m in range(1, NP):
-        back_copy(1, m, True).wait_recv()
-        ra_exp[m] = rb_exp[m]
-    for m in range(1, NP):
-        back_copy(0, m, True).wait_recv()
-        ra_in[m] = rb_in[m]
-    for i in range(1, NZ):
-        sz_copy(i, True).wait_recv()
+    leave(tout_ref, tout_out)
+    back_group(1).wait_recv()
+    leave(rb_exp.at[pl.ds(1, NP - 1)], exp_out.at[pl.ds(1, NP - 1)])
+    back_group(0).wait_recv()
+    leave(rb_in.at[pl.ds(1, NP - 1)], in_out.at[pl.ds(1, NP - 1)])
+    sz_group = bundle(rzv.at[pl.ds(1, NZ - 1)], sz_s.at[0], sz_r.at[0])
+    sz_group.wait_recv()
     tile = zt[d]
     for i in range(1, NZ):
         tile = tile + rzv[i]
     tile_ref[...] = jnp.where(rows8 == 3, tile, pltpu.roll(tile, lax.rem(128 - 32 * quad, 128), 1))
 
-    for m in range(1, NP):
-        a2a_msg(0, m).wait_send()
-        a2a_msg(1, m).wait_send()
-        vp_copy(m, False).wait_send()
-        back_copy(0, m, False).wait_send()
-        back_copy(1, m, False).wait_send()
-        sp_copy(m).wait_send()
-    for m in range(1, 4):
-        wo_copy(m, False).wait_send()
-        go_copy(m, False).wait_send()
-    for i in range(1, NZ):
-        vz_copy(i, False).wait_send()
-        sz_copy(i, False).wait_send()
-    for i in range(9):
-        ag_copy(1, i, False).wait_send()
+    for out in leaving:
+        out.wait()
     for w in range(2):
-        for i in range(10):
-            rs_copy(w, i).wait_send()
+        a2a_group(w).wait_send()
+        back_group(w).wait_send()
+    for g in (vz_group, vp_group, wo_group, go_group, sp_group, sz_group):
+        g.wait_send()
+    ag_sent(1)
+    for w in range(2):
+        bundle(RS[w][0].at[pl.ds(0, 7 * rows)], rs_s.at[w], rs_r.at[w, 0]).wait_send()
     for a in range(4):
         z_sent(a)
         zr_sent(a)
@@ -1260,10 +1276,11 @@
         vm((NP, 32, 384), BF16), vm((NP, 32, ff), BF16),
         vm((NP, NZ, 8, 128), F32), vm((8, D), F32), vm((8, ff), F32), vm((8, ff), F32), vm((8, D), F32),
         vm((2, NZ, 8, 128), F32), vm((NP, NZ, 8, 128), F32), vm((NZ, 8, 128), F32), vm((NZ, 8, 128), F32),
-        dma((2, NP)), dma((2, NP)), dma((2, 9)), dma((2, 9)), dma((4, 5)), dma((4, 4)),
-        dma((NZ,)), dma((NZ,)), dma((NP,)), dma((NP,)), dma((4,)), dma((4,)),
-        dma((2, 10)), dma((2, 10)), dma((4, 4)), dma((4, 4)), dma((4,)), dma((4,)),
-        dma((2, NP)), dma((2, NP)), dma((NP,)), dma((NP,)), dma((NZ,)), dma((NZ,)), dma,
+        dma((2,)), dma((2,)), dma((2,)), dma((2, 9)), dma((4,)), dma((4, 4)),
+        dma((1,)), dma((1,)), dma((1,)), dma((1,)), dma((1,)), dma((1,)),
+        dma((2,)), dma((2, 10)), dma((4,)), dma((4, 4)), dma((1,)), dma((1,)),
+        dma((2,)), dma((2,)), dma((1,)), dma((1,)), dma((1,)), dma((1,)), dma,
+        vm((rows, D), BF16), vm((rows, D), BF16), vm((128, D), F32), vm((32, D), F32), dma((8,)),
     ]
     in_vmem = pl.BlockSpec(memory_space=pltpu.VMEM)
     in_smem = pl.BlockSpec(memory_space=pltpu.SMEM)
@@ -1281,7 +1298,7 @@
             jax.ShapeDtypeStruct((8, 128), F32),
         ],
         in_specs=[in_vmem, pl.BlockSpec(memory_space=pl.ANY)] + [in_vmem] * 12,
-        out_specs=[in_vmem] * 7,
+        out_specs=[pl.BlockSpec(memory_space=pl.ANY)] * 6 + [in_vmem],
         scratch_shapes=scratch,
         compiler_params=pltpu.CompilerParams(
             collective_id=0, has_side_effects=True, vmem_limit_bytes=63 * 2**20

time: 138 us -> 135 us (0.978); the launches traced: 135 us -> 134 us
  no operation moved by 1% of the time
where the time goes in v4:
time: 135 us; the launch traced here: 134 us
  Pallas kernels  132 us (98%)
  between operations  2.13 us (2%)
    pallas_call x1, Pallas kernels, fused_shards(): pl.pallas_call(body, out_shape=[rows_shape, rows_shape, jax.ShapeDtypeStr...  126 us
    pallas_call x1, Pallas kernels, fused_shards(): pl.pallas_call(update_kernel, out_shape=[rows_shape, rows_shape] + shard_...  5.19 us

profile of v4, /device:TPU:13, one launch (start us, length us, event | category | flops | bytes accessed | tf_op | source)
XLA Modules:
  0.0 133.8 jit_solution(16626574911096018142)
XLA Ops:
  1.9 126.5 %block_step.1 = (bf16[256,1024]{1,0:T(8,128)(2,1)}, bf16[256,1024]{1,0:T(8,128)(2,1)}, bf16[8,32,384]{2,1,0:T(8,128)(2,1)}, bf16[8,32,512]{2,1,0:T(8,128)(2,1)},...) custom-call(bf16[256,1024]{1,0:T(8,128)(2,1)} %bitcast.20, bf16[256,1024]{1,0:T(8,128)(2,1)} %bitcast.21, ...), custom_call_target="tpu_custom_call" | custom-call | tf_op jit(solution)/shard_map/block_step/pallas_call | solution.py:1292
  128.4 5.2 %block_update.1 = (bf16[256,1024]{1,0:T(8,128)(2,1)}, bf16[256,1024]{1,0:T(8,128)(2,1)}, f32[1,32]{1,0:T(1,128)}, f32[1,32]{1,0:T(1,128)}, f32[32,3072]{1,0:T(8,...) custom-call(f32[1,32]{1,0:T(1,128)} %bitcast.23, ...), custom_call_target="tpu_custom_call" | custom-call | tf_op jit(solution)/shard_map/block_update/pallas_call | solution.py:1310

commit v5 on v4

--- a/solution.py
+++ b/solution.py
@@ -592,11 +592,11 @@
 
     def norm_block(b):
         def step(c, carry):
-            at = aligned(rows * b + 64 * c, 64)
-            unit, _ = unit_of(xg[pl.ds(at, 64), :])
-            xn[pl.ds(at, 64), :] = (unit * vecs[0:1, :] + vecs[1:2, :]).astype(BF16)
+            at = aligned(rows * b + 128 * c, 128)
+            unit, _ = unit_of(xg[pl.ds(at, 128), :])
+            xn[pl.ds(at, 128), :] = (unit * vecs[0:1, :] + vecs[1:2, :]).astype(BF16)
             return carry
-        lax.fori_loop(0, rows // 64, step, 0)
+        lax.fori_loop(0, rows // 128, step, 0)
 
     lane_b = lax.broadcasted_iota(jnp.int32, (rows, 128), 1)
     low_head = lane_b < HD

time: 135 us -> 135 us (level)
  no operation moved by 1% of the time
where the time goes in v5:
time: 135 us; the launch traced here: 134 us
  Pallas kernels  132 us (98%)
  between operations  2.13 us (2%)
    pallas_call x1, Pallas kernels, fused_shards(): pl.pallas_call(body, out_shape=[rows_shape, rows_shape, jax.ShapeDtypeStr...  126 us
    pallas_call x1, Pallas kernels, fused_shards(): pl.pallas_call(update_kernel, out_shape=[rows_shape, rows_shape] + shard_...  5.19 us

profile of v5, /device:TPU:13, one launch (start us, length us, event | category | flops | bytes accessed | tf_op | source)
XLA Modules:
  0.0 133.8 jit_solution(8284785769714897118)
XLA Ops:
  1.9 126.5 %block_step.1 = (bf16[256,1024]{1,0:T(8,128)(2,1)}, bf16[256,1024]{1,0:T(8,128)(2,1)}, bf16[8,32,384]{2,1,0:T(8,128)(2,1)}, bf16[8,32,512]{2,1,0:T(8,128)(2,1)},...) custom-call(bf16[256,1024]{1,0:T(8,128)(2,1)} %bitcast.20, bf16[256,1024]{1,0:T(8,128)(2,1)} %bitcast.21, ...), custom_call_target="tpu_custom_call" | custom-call | tf_op jit(solution)/shard_map/block_step/pallas_call | solution.py:1292
  128.4 5.2 %block_update.1 = (bf16[256,1024]{1,0:T(8,128)(2,1)}, bf16[256,1024]{1,0:T(8,128)(2,1)}, f32[1,32]{1,0:T(1,128)}, f32[1,32]{1,0:T(1,128)}, f32[32,3072]{1,0:T(8,...) custom-call(f32[1,32]{1,0:T(1,128)} %bitcast.23, ...), custom_call_target="tpu_custom_call" | custom-call | tf_op jit(solution)/shard_map/block_update/pallas_call | solution.py:1310
